TPU v7x, 512 devices: a whole 4x8x8 slice. The times are simulated.
512 devices in a mesh: cfg: 2 (over z_lo), rs: 32 (over x, z_hi, core), tp: 8 (over y).
Axes of the slice: x: 4, y: 8, z: 8 (z_hi: 4, z_lo: 2; z = z_hi * 2 + z_lo), core: 2. Of those that a mesh axis runs over, the one named last changes fastest.
Arguments:
- latents: float32 [8192, 2, 16], P('rs'), may hold values from -6 to 6
- timesteps: int32 [8, 2], replicated, may hold values from 0 to 249
- labels: int32 [8, 2], replicated, may hold values from 0 to 999
- solver_table: float32 [250, 2], replicated, may hold values from 0.5 to 1.5
- time_table: bfloat16 [250, 1152], P(None, 'tp'), may hold values from -6 to 6
- label_table: bfloat16 [1001, 1152], P(None, 'tp'), may hold values from -6 to 6
- patch_weight: bfloat16 [16, 1152], replicated, may hold values from -1.5 to 1.5
- patch_bias: float32 [1152], replicated, may hold values from -3 to 3
- modulation_weight: bfloat16 [9216, 1152], P(('rs', 'tp')), may hold values from -0.1875 to 0.1875
- modulation_bias: float32 [9216], P(('rs', 'tp')), may hold values from -3 to 3
- heads_weight: bfloat16 [1, 1152, 3, 1152], P(None, None, None, 'tp'), may hold values from -0.375 to 0.375
- heads_bias: float32 [1, 3, 1152], P(None, None, 'tp'), may hold values from -1.75 to 1.75
- output_weight: bfloat16 [1, 1152, 1152], P(None, 'tp'), may hold values from -0.1875 to 0.1875
- output_bias: float32 [1, 1152], replicated, may hold values from -1.75 to 1.75
- up_weight: bfloat16 [1, 1152, 4608], P(None, None, 'tp'), may hold values from -0.1875 to 0.1875
- up_bias: float32 [1, 4608], P(None, 'tp'), may hold values from -1.75 to 1.75
- down_weight: bfloat16 [1, 4608, 1152], P(None, 'tp'), may hold values from -0.09375 to 0.09375
- down_bias: float32 [1, 1152], replicated, may hold values from -1.75 to 1.75
- final_weight: bfloat16 [1152, 16], replicated, may hold values from -0.1875 to 0.1875
- final_bias: float32 [16], replicated, may hold values from -1.75 to 1.75
Outputs:
- next_latents: float32 [8192, 2, 16], P(('rs', 'tp'), None, 'cfg')
All inputs are finite; a program needn't handle non-finite values.
Results may differ from a plain program's by a relative error of at most 0.02.
Values may be sent and summed in bfloat16 or wider, within the bound.
A program may use at most 64 MiB of HBM per device.

v0:
```python
import jax
import jax.numpy as jnp
from jax import lax
from jax.sharding import PartitionSpec as P

HEAD_DIM = 72
GRID = 32
LAYERS = 1


guidance = 4.0


def partner_2(value, axis, stride):
    mask = 2**stride
    pairs = [(source, source ^ mask) for source in range(lax.axis_size(axis))]
    return lax.ppermute(value, axis, pairs)


def layer_norm(values):
    centre = values - jnp.mean(values, axis=-1, keepdims=True)
    spread = jnp.mean(centre * centre, axis=-1, keepdims=True)
    return centre * lax.rsqrt(spread + 1e-06)


def position_rows(token_index, grid_side, model_width):
    freq_count = model_width // 4
    frequency = 1.0 / 10000.0 ** (jnp.arange(freq_count, dtype=jnp.float32) / freq_count)
    row_angle = (token_index // grid_side).astype(jnp.float32)[:, None] * frequency[None, :]
    col_angle = (token_index % grid_side).astype(jnp.float32)[:, None] * frequency[None, :]
    return jnp.concatenate(
        [jnp.sin(row_angle), jnp.cos(row_angle), jnp.sin(col_angle), jnp.cos(col_angle)], axis=1
    )


def modulate(stream, modulation, offset):
    return (
        layer_norm(stream) * (1.0 + modulation[None, :, offset + 1]) + modulation[None, :, offset]
    ).astype(jnp.bfloat16)


def project_heads(normed, weight, bias):
    row_count, latents_dev, model_width = normed.shape
    flattened = normed.reshape(row_count * latents_dev, model_width)
    result = jnp.dot(
        flattened, weight.reshape(model_width, -1), preferred_element_type=jnp.float32
    ) + bias.reshape(-1)
    return result.astype(jnp.bfloat16).reshape(row_count, latents_dev, -1)


def hidden_units(normed, weight, bias):
    row_count, latents_dev, model_width = normed.shape
    flattened = normed.reshape(row_count * latents_dev, model_width)
    preact = jnp.dot(flattened, weight, preferred_element_type=jnp.float32) + bias
    return (
        jax.nn.gelu(preact, approximate=True)
        .astype(jnp.bfloat16)
        .reshape(row_count, latents_dev, -1)
    )


def attend_block(queries, key_block, columns):
    key_count, latents_dev = (key_block.shape[0], key_block.shape[1])
    head_count, head_size = (queries.shape[2], queries.shape[3])
    key_rows = key_block[..., :columns].reshape(key_count, latents_dev, head_count, head_size)
    value_rows = key_block[..., columns:].reshape(key_count, latents_dev, head_count, head_size)
    scores = jnp.einsum(
        "qlhd,klhd->lhqk", queries, key_rows, preferred_element_type=jnp.float32
    ) * head_size ** (-0.5)
    row_top = jnp.max(scores, axis=-1)
    exponent = jnp.exp(scores - row_top[..., None])
    row_total = jnp.sum(exponent, axis=-1)
    weighted = jnp.einsum(
        "lhqk,klhd->lhqd",
        exponent.astype(jnp.bfloat16),
        value_rows,
        preferred_element_type=jnp.float32,
    )
    return (row_top, row_total, weighted)


def merge_blocks(first, second):
    row_top = jnp.maximum(first[0], second[0])
    left_scale = jnp.exp(first[0] - row_top)
    right_scale = jnp.exp(second[0] - row_top)
    row_total = first[1] * left_scale + second[1] * right_scale
    weighted = first[2] * left_scale[..., None] + second[2] * right_scale[..., None]
    return (row_top, row_total, weighted)


def attention(projected, columns, head_size):
    row_count, latents_dev = (projected.shape[0], projected.shape[1])
    queries = projected[..., :columns].reshape(
        row_count, latents_dev, columns // head_size, head_size
    )
    own_block = projected[..., columns:]
    running = attend_block(queries, own_block, columns)
    near_block = partner_2(own_block, "rs", 0)
    running = merge_blocks(running, attend_block(queries, near_block, columns))
    far_block = partner_2(jnp.concatenate([own_block, near_block], axis=0), "rs", 1)
    running = merge_blocks(running, attend_block(queries, far_block, columns))
    result = running[2] / running[1][..., None]
    return (
        jnp.transpose(result, (2, 0, 1, 3))
        .reshape(row_count, latents_dev, columns)
        .astype(jnp.bfloat16)
    )


def per_device(
    latents,
    timesteps,
    labels,
    solver_table,
    time_table,
    label_table,
    patch_weight,
    patch_bias,
    modulation_weight,
    modulation_bias,
    heads_weight,
    heads_bias,
    output_weight,
    output_bias,
    up_weight,
    up_bias,
    down_weight,
    down_bias,
    final_weight,
    final_bias,
):
    tp_count = lax.axis_size("tp")
    tp_index = lax.axis_index("tp")
    half_index = lax.axis_index("cfg")
    rs_index = lax.axis_index("rs")
    group_index = rs_index // 4
    quarter = rs_index % 4
    local_tokens, latents_dev, patch_width = latents.shape
    model_width = patch_weight.shape[1]
    share_rows = local_tokens // tp_count
    classes = label_table.shape[0] - 1
    columns = heads_weight.shape[3]
    steps_all = timesteps.reshape(-1)
    class_ids = jnp.where(half_index == 0, labels.reshape(-1), classes)
    step_onehot = jax.nn.one_hot(steps_all, time_table.shape[0], dtype=jnp.bfloat16)
    class_onehot = jax.nn.one_hot(class_ids, classes + 1, dtype=jnp.bfloat16)
    condition_part = jnp.dot(step_onehot, time_table, preferred_element_type=jnp.float32) + jnp.dot(
        class_onehot, label_table, preferred_element_type=jnp.float32
    )
    condition = lax.all_gather(condition_part, "tp", axis=1, tiled=True)
    activation = jax.nn.silu(condition).astype(jnp.bfloat16)
    modulation_part = (
        lax.dot_general(
            activation,
            modulation_weight,
            (((1,), (1,)), ((), ())),
            preferred_element_type=jnp.float32,
        )
        + modulation_bias
    )
    modulation_all = lax.all_gather(modulation_part, ("rs", "tp"), axis=1, tiled=True)
    modulation_all = modulation_all.reshape(timesteps.shape[0], latents_dev, -1, model_width)
    modulation = lax.dynamic_index_in_dim(modulation_all, group_index, 0, keepdims=False)
    token_index = quarter * local_tokens + jnp.arange(local_tokens, dtype=jnp.int32)
    position = position_rows(token_index, GRID, model_width)
    own_latents = lax.dynamic_slice_in_dim(latents, tp_index * share_rows, share_rows, 0)
    flattened = latents.reshape(-1, patch_width).astype(jnp.bfloat16)
    embedded = jnp.dot(flattened, patch_weight, preferred_element_type=jnp.float32) + patch_bias
    stream = embedded.reshape(latents.shape[0], latents_dev, model_width) + position[:, None, :]
    projected = project_heads(modulate(stream, modulation, 0), heads_weight[0], heads_bias[0])
    attended = attention(projected, columns, HEAD_DIM).reshape(-1, columns)
    head_terms = jnp.dot(attended, output_weight[0], preferred_element_type=jnp.float32)
    attn_out = (
        lax.psum(head_terms.astype(jnp.bfloat16), "tp")
        .astype(jnp.float32)
        .reshape(local_tokens, latents_dev, model_width)
    )
    stream = stream + modulation[None, :, 2] * (attn_out + output_bias[0])
    hidden = hidden_units(modulate(stream, modulation, 3), up_weight[0], up_bias[0])
    unit_terms = jnp.dot(
        hidden.reshape(-1, hidden.shape[2]), down_weight[0], preferred_element_type=jnp.float32
    )
    mlp_out = (
        lax.psum(unit_terms.astype(jnp.bfloat16), "tp")
        .astype(jnp.float32)
        .reshape(local_tokens, latents_dev, model_width)
    )
    stream = stream + modulation[None, :, 5] * (mlp_out + down_bias[0])
    own_stream = lax.dynamic_slice_in_dim(stream, tp_index * share_rows, share_rows, 0)
    final_normed = modulate(own_stream, modulation, 6 * LAYERS)
    noise_pred = (
        jnp.dot(
            final_normed.reshape(-1, model_width), final_weight, preferred_element_type=jnp.float32
        )
        + final_bias
    )
    noise_pred = noise_pred.reshape(share_rows, latents_dev, patch_width)
    half_width = patch_width // 2
    kept_half = lax.dynamic_slice_in_dim(noise_pred, half_index * half_width, half_width, 2)
    sent_half = lax.dynamic_slice_in_dim(noise_pred, (1 - half_index) * half_width, half_width, 2)
    partner = partner_2(sent_half, "cfg", 0)
    conditional = jnp.where(half_index == 0, kept_half, partner)
    unconditional = jnp.where(half_index == 0, partner, kept_half)
    guided = unconditional + guidance * (conditional - unconditional)
    own_channels = lax.dynamic_slice_in_dim(own_latents, half_index * half_width, half_width, 2)
    step_own = lax.dynamic_index_in_dim(timesteps, group_index, 0, keepdims=False)
    step_hot_own = jax.nn.one_hot(step_own, solver_table.shape[0], dtype=jnp.float32)
    coefficients = jnp.dot(step_hot_own, solver_table, precision=lax.Precision.HIGHEST)
    return coefficients[None, :, 0:1] * own_channels + coefficients[None, :, 1:2] * guided


def solution(mesh):
    in_specs = (
        P("rs", None, None),
        P(),
        P(),
        P(),
        P(None, "tp"),
        P(None, "tp"),
        P(),
        P(),
        P(("rs", "tp"), None),
        P(("rs", "tp")),
        P(None, None, None, "tp"),
        P(None, None, "tp"),
        P(None, "tp", None),
        P(),
        P(None, None, "tp"),
        P(None, "tp"),
        P(None, "tp", None),
        P(),
        P(),
        P(),
    )
    out_specs = P(("rs", "tp"), None, "cfg")
    return jax.shard_map(
        per_device, mesh=mesh, in_specs=in_specs, out_specs=out_specs, check_vma=False
    )
```

profile of v0, /device:TPU:4, one launch (start us, length us, event | category | flops | bytes accessed | tf_op | source)
XLA Modules:
  0.0 997.7 jit_solution(18414856131837989022)
XLA Ops:
  6.6 3.8 multiply_cosine_fusion
  12.0 2.2 add.308
  14.2 4.0 add.314
  18.4 3.6 fusion.90
  24.6 26.2 %all-gather = f32[8,144,16]{1,2,0:T(8,128)S(1)} all-gather(f32[1,144,16]{1,2,0:T(8,128)S(1)} %fusion.29), channel_id=1, replica_groups=mesh['cfg'=2,'rs'=32,'tp'=8] {'tp'}, dimensions={0}, use_global_device_ids=true | all-gather | bytes 82944 | tf_op jit(solution)/shard_map/all_gather | solution.py:150
  51.2 616.9 %all-gather.1 = f32[256,36,16]{1,2,0:T(8,128)S(1)} all-gather(f32[1,36,16]{1,2,0:T(8,128)S(1)} %fusion.30), channel_id=1, replica_groups=mesh['cfg'=2,'rs'=32,'tp'=8] {'rs','tp'}, dimensions={0}, use_global_device_ids=true | all-gather | bytes 592128 | tf_op jit(solution)/shard_map/all_gather | solution.py:161
  668.8 2.4 reshape.290
  675.1 4.0 add.321
  681.2 4.1 mul.285
  685.5 4.1 fusion.4
  696.6 2.2 pad_maximum_fusion
  700.9 2.1 collective-permute-start.1
  706.1 26.2 %collective-permute-done.1 = bf16[512,2,288]{0,2,1:T(8,128)(2,1)} collective-permute-done((bf16[512,2,288]{0,2,1:T(8,128)(2,1)}, bf16[512,2,288]{0,2,1:T(8,128)(2,1)}, u32[]{:S(2)}, u32[]{:S(2)}) %collective-permute-start.1) | collective-permute-done | bytes 589856 | tf_op jit(solution)/shard_map/ppermute | solution.py:17
  739.9 4.1 mul.306
  744.0 2.1 add.341
  746.1 4.0 add.342
  752.2 4.1 mul.312
  756.2 132.5 %all-reduce.3.cloned.1.call-done = bf16[512,1152]{1,0:T(8,128)(2,1)} async-done(((bf16[512,1152]{1,0:T(8,128)(2,1)}), bf16[512,1152]{1,0:T(8,128)(2,1)}) %all-reduce.3.cloned.1.call-update) | async-done | bytes 1179664 | tf_op jit(solution)/shard_map/psum | solution.py:174
  888.7 3.2 fusion.85
  893.7 5.7 convolution_convert_fusion.1
  901.0 4.1 reshape.272
  906.3 2.2 reshape.282
  908.5 73.4 %all-reduce.5.cloned.1.call-done = bf16[256,2,1152]{2,1,0:T(2,128)(2,1)} async-done(((bf16[256,2,1152]{2,1,0:T(2,128)(2,1)}), bf16[256,2,1152]{2,1,0:T(2,128)(2,1)}) %all-reduce.5.cloned.1.call-update) | async-done | bytes 1179664 | tf_op jit(solution)/shard_map/psum | solution.py:184
  984.6 3.6 collective-permute-start.2
  (144 shorter events, 42.9 us)
Async XLA Ops:
  6.5 887.2 %copy-start = (bf16[1,576,1152]{2,1,0:T(8,128)(2,1)S(1)}, bf16[1,576,1152]{2,1,0:T(8,128)(2,1)}, u32[]{:S(2)}) copy-start(bf16[1,576,1152]{2,1,0:T(8,128)(2,1)} %param.36) | copy-start | bytes 3981316
  6.5 882.2 %all-reduce.3.cloned.1.call-start = ((), (), s32[]{:S(2)}) async-start(), calls=%async_computation | async-start | bytes 2359296 | tf_op jit(solution)/shard_map/psum | solution.py:174
  12.0 6.3 copy-start.3
  14.2 4.1 copy-start.10
  14.2 4.2 copy-start.11
  14.2 4.2 copy-start.14
  22.1 2.3 copy-start.8
  22.1 28.9 %copy-start.22 = (bf16[36,1152]{1,0:T(8,128)(2,1)S(1)}, bf16[36,1152]{1,0:T(8,128)(2,1)}, u32[]{:S(2)}) copy-start(bf16[36,1152]{1,0:T(8,128)(2,1)} %param.28) | copy-start | bytes 248836
  22.1 28.9 %copy-start.26 = (f32[36]{0:T(128)S(1)}, f32[36]{0:T(128)}, u32[]{:S(2)}) copy-start(f32[36]{0:T(128)} %param.29) | copy-start | bytes 436
  681.2 4.1 copy-start.19
  681.2 4.2 copy-start.6
  690.7 5.9 copy-start.5
  690.7 5.9 collective-permute-start
  700.9 31.5 %collective-permute-start.1 = (bf16[512,2,288]{0,2,1:T(8,128)(2,1)}, bf16[512,2,288]{0,2,1:T(8,128)(2,1)}, u32[]{:S(2)}, u32[]{:S(2)}) collective-permute-start(bf16[512,2,288]{0,2,1:T(8,128)(2,1)} %copy.84), channel_id=1, source_target_pairs={{0,16},{8,24},{16,0},{24,8},{32,48},{40,56},{48,32},{56,40},{64,80... | collective-permute-start | bytes 1769480 | tf_op jit(solution)/shard_map/ppermute | solution.py:17
  737.8 244.1 %all-reduce.5.cloned.1.call-start = ((), (), s32[]{:S(2)}) async-start(), calls=%async_computation.1 | async-start | bytes 2359296 | tf_op jit(solution)/shard_map/psum | solution.py:184
  739.9 4.1 copy-start.15
  739.9 4.1 copy-start.12
  752.2 4.1 copy-start.20
  901.0 4.1 copy-start.16
  901.0 4.1 copy-start.25
  901.0 5.2 copy-start.4
  906.3 77.9 %copy-start.24 = (bf16[1152,16]{0,1:T(8,128)(2,1)S(1)}, bf16[1152,16]{0,1:T(8,128)(2,1)}, u32[]{:S(2)}) copy-start(bf16[1152,16]{0,1:T(8,128)(2,1)} %param.38) | copy-start | bytes 110596
  906.3 77.9 %copy-start.27 = (f32[16]{0:T(128)S(1)}, f32[16]{0:T(128)}, u32[]{:S(2)}) copy-start(f32[16]{0:T(128)} %param.39) | copy-start | bytes 196
  984.6 5.5 collective-permute-start.2
  (9 other events, 13.6 us)
Sparse Core Ops, SparseCore 0:
  737.9 150.7 all-reduce.2
  900.9 80.9 all-reduce.4
where the time goes:
time: 999 us; the launch traced here: 998 us
  blocking collectives  643 us (64%)
  waiting for transfers between devices  234 us (23%)
  local copies, waits for them, and re-layouts  64.7 us (6%)
  matrix products  19.2 us (2%)
  other arithmetic  15.1 us (2%)
  between operations  14 us (1%)
    all_gather x1, blocking collectives, per_device(): lax.all_gather(modulation_part, ('rs', 'tp'), axis=1, tiled=True)  617 us
    psum x1, waiting for transfers between devices, per_device(): lax.psum(head_terms.astype(jnp.bfloat16), 'tp').astype(jnp.float32)  133 us
    psum x1, waiting for transfers between devices, per_device(): lax.psum(unit_terms.astype(jnp.bfloat16), 'tp').astype(jnp.float32)  73.4 us
    ppermute x3, waiting for transfers between devices, partner_2(): return lax.ppermute(value, axis, pairs)  28 us
    all_gather x1, blocking collectives, per_device(): condition = lax.all_gather(condition_part, 'tp', axis=1, tiled=True)  26.2 us
  transfers between devices with their start and end apart: 5, of which 4 were waited for; matrix products, arithmetic and copies ran while one was open for 3% of the time, Pallas kernels for 0%

commit v1 on v0

v1 whole, which is shorter than its diff:
```python
import functools

import jax
import jax.numpy as jnp
import numpy as np
from jax import lax
from jax.experimental import pallas as pl
from jax.experimental.pallas import tpu as pltpu
from jax.sharding import PartitionSpec as P

HEAD_DIM = 72
GRID = 32
D = 1152
LANES = 128
GUIDANCE = 4.0
MESH = pl.DeviceIdType.MESH
F32, BF16 = jnp.float32, jnp.bfloat16


def remote(src, dst, send, recv, device):
    return pltpu.make_async_remote_copy(
        src_ref=src, dst_ref=dst, send_sem=send, recv_sem=recv, device_id=device, device_id_type=MESH
    )


def layer_norm(values):
    centre = values - jnp.mean(values, axis=-1, keepdims=True)
    spread = jnp.mean(centre * centre, axis=-1, keepdims=True)
    return centre * lax.rsqrt(spread + 1e-06)


def position_tables():
    count = D // 4
    frequency = 1.0 / 10000.0 ** (np.arange(count, dtype=np.float64) / count)
    angle = np.arange(GRID, dtype=np.float64)[:, None] * frequency[None, :]
    half = np.concatenate([np.sin(angle), np.cos(angle)], axis=1)
    zero = np.zeros_like(half)
    row = np.concatenate([half, zero], axis=1).astype(np.float32)
    col = np.concatenate([zero, half], axis=1).astype(np.float32)
    return row, col


def conditioning_kernel(
    tp_n, rs_n, cond_ref, w_ref, b_ref, lat_ref, out_ref, latall_ref,
    cbuf, part, pbuf, blk, obuf, lbuf, s1, r1, s2, r2, s3, r3, s4, r4,
):
    tp, rs = lax.axis_index("tp"), lax.axis_index("rs")
    quarter, base = rs % 4, (rs // 4) * 4
    barrier = pltpu.get_barrier_semaphore()
    for d in range(1, tp_n):
        pl.semaphore_signal(barrier, inc=1, device_id={"tp": (tp + d) % tp_n}, device_id_type=MESH)
    for d in range(1, rs_n):
        pl.semaphore_signal(barrier, inc=1, device_id={"rs": (rs + d) % rs_n}, device_id_type=MESH)
    pl.semaphore_wait(barrier, tp_n - 1 + rs_n - 1)

    first = []
    for d in range(1, tp_n):
        c = remote(cond_ref, cbuf.at[tp], s1.at[d], r1.at[d], {"tp": (tp + d) % tp_n})
        c.start()
        first.append(c)
    lats = []
    for d in range(1, 4):
        c = remote(lat_ref, lbuf.at[d], s4.at[d], r4.at[d], {"rs": base + (quarter + d) % 4})
        c.start()
        lats.append(c)
    cbuf[tp] = cond_ref[...]
    for c in first:
        c.wait()
    total = jnp.broadcast_to(b_ref[...], (cond_ref.shape[0], LANES))
    for t in range(tp_n):
        v = cbuf[t]
        act = (v / (1.0 + jnp.exp(-v))).astype(BF16)
        total = total + lax.dot_general(
            act, w_ref[t], (((1,), (1,)), ((), ())), preferred_element_type=F32
        )
    part[...] = total
    second = []
    for d in range(1, tp_n):
        c = remote(part, pbuf.at[tp], s2.at[d], r2.at[d], {"tp": (tp + d) % tp_n})
        c.start()
        second.append(c)
    pbuf[tp] = total
    for c in second:
        c.wait()
    share = D * 8 // (tp_n * rs_n)
    rows = jnp.concatenate([pbuf[t][:, :share] for t in range(tp_n)], axis=1)
    for g in range(blk.shape[0]):
        blk[g, :, : rows.shape[1]] = rows[2 * g : 2 * g + 2, :]
    third = []
    for d in range(1, rs_n):
        peer = (rs + d) % rs_n
        c = remote(blk.at[peer // 4], obuf.at[rs], s3.at[d], r3.at[d], {"rs": peer})
        c.start()
        third.append(c)
    obuf[rs] = blk[rs // 4]
    latall_ref[0] = lat_ref[...]
    for d in range(1, 4):
        lats[d - 1].wait()
        latall_ref[d] = lbuf[d]
    for c in third:
        c.wait()
    out_ref[...] = obuf[...]


def conditioning(cond, weight, bias, lat, tp_n, rs_n):
    n = cond.shape[0]
    wide = 3 * LANES
    vmem = pl.BlockSpec(memory_space=pltpu.VMEM)
    dma = pltpu.SemaphoreType.DMA
    return pl.pallas_call(
        functools.partial(conditioning_kernel, tp_n, rs_n),
        out_shape=(
            jax.ShapeDtypeStruct((rs_n, 2, wide), F32),
            jax.ShapeDtypeStruct((4,) + lat.shape, BF16),
        ),
        in_specs=[vmem] * 4,
        out_specs=(vmem, vmem),
        scratch_shapes=[
            pltpu.VMEM((tp_n,) + cond.shape, F32),
            pltpu.VMEM((n, LANES), F32),
            pltpu.VMEM((tp_n, n, LANES), F32),
            pltpu.VMEM((n // 2, 2, wide), F32),
            pltpu.VMEM((rs_n, 2, wide), F32),
            pltpu.VMEM((4,) + lat.shape, BF16),
            dma((tp_n,)), dma((tp_n,)), dma((tp_n,)), dma((tp_n,)),
            dma((rs_n,)), dma((rs_n,)), dma((4,)), dma((4,)),
        ],
        compiler_params=pltpu.CompilerParams(collective_id=0, has_side_effects=True),
        name="conditioning",
    )(cond, weight, bias, lat)


def attention_kernel(lat_ref, pw_ref, col_ref, row_ref, mod_ref, wq_ref, wkv_ref, bq_ref, bkv_ref,
                     wo_ref, out_ref, normed, kv):
    tile = 256

    def fill(step, latent, slot):
        emb = jnp.dot(
            lat_ref[latent, pl.ds(pl.multiple_of(slot * tile, tile), tile), :],
            pw_ref[...], preferred_element_type=F32,
        )
        shift, scale = mod_ref[latent, 0:1, :], 1.0 + mod_ref[latent, 1:2, :]
        for i in range(tile // GRID):
            stream = (emb[i * GRID : (i + 1) * GRID] + col_ref[...]) + row_ref[slot, i : i + 1, :]
            normed[i * GRID : (i + 1) * GRID, :] = (
                layer_norm(stream) * scale + shift
            ).astype(BF16)
        pair = jnp.dot(normed[...], wkv_ref[...], preferred_element_type=F32) + bkv_ref[...]
        kv[pl.ds(pl.multiple_of(slot * tile, tile), tile), :] = pair.astype(BF16)

    @pl.loop(0, 2)
    def _(latent):
        @pl.loop(0, 4)
        def _(step):
            fill(step, latent, 3 - step)

        queries = (
            jnp.dot(normed[...], wq_ref[...], preferred_element_type=F32) + bq_ref[...]
        ).astype(BF16)
        total = None
        for h in range(2):
            q = queries[:, h * LANES : (h + 1) * LANES]
            k = kv[:, h * LANES : (h + 1) * LANES]
            v = kv[:, (2 + h) * LANES : (3 + h) * LANES]
            scores = lax.dot_general(
                q, k, (((1,), (1,)), ((), ())), preferred_element_type=F32
            ) * HEAD_DIM ** (-0.5)
            exponent = jnp.exp(scores - jnp.max(scores, axis=-1, keepdims=True))
            row_total = jnp.sum(exponent, axis=-1, keepdims=True)
            weighted = jnp.dot(exponent.astype(BF16), v, preferred_element_type=F32)
            attended = (weighted / row_total).astype(BF16)
            term = jnp.dot(attended, wo_ref[h], preferred_element_type=F32)
            total = term if total is None else total + term
        result = total.astype(BF16)
        for t in range(8):
            out_ref[t, latent] = result[t * GRID : (t + 1) * GRID, :]


def attention(lat, pw, col, row, mod, wq, wkv, bq, bkv, wo):
    vmem = pl.BlockSpec(memory_space=pltpu.VMEM)
    return pl.pallas_call(
        attention_kernel,
        out_shape=jax.ShapeDtypeStruct((8, 2, GRID, D), BF16),
        in_specs=[vmem] * 10,
        out_specs=vmem,
        scratch_shapes=[pltpu.VMEM((256, D), BF16), pltpu.VMEM((1024, 4 * LANES), BF16)],
        compiler_params=pltpu.CompilerParams(vmem_limit_bytes=60000000),
        name="attention",
    )(lat, pw, col, row, mod, wq, wkv, bq, bkv, wo)


def feed_kernel(
    n, part_ref, lat_ref, latb_ref, pw_ref, pos_ref, mod_ref, ob_ref, up_ref, upb_ref, down_ref,
    downb_ref, fw_ref, fb_ref, c0_ref, c1_ref, out_ref,
    r1, gathered, held, r2, stream_ref, own, noise, other,
    s1, q1, sr, qr, sl, ql, s2, q2, s3, q3,
):
    me, half = lax.axis_index("tp"), lax.axis_index("cfg")
    barrier = pltpu.get_barrier_semaphore()
    for d in range(1, n):
        pl.semaphore_signal(barrier, inc=1, device_id={"tp": (me + d) % n}, device_id_type=MESH)
    pl.semaphore_signal(barrier, inc=1, device_id={"cfg": 1 - half}, device_id_type=MESH)
    pl.semaphore_wait(barrier, n)

    sent = []
    for d in (4, 3, 5, 2, 6, 1, 7):
        peer = (me + d) % n
        c = remote(part_ref.at[peer], r1.at[d], s1.at[d], q1.at[d], {"tp": peer})
        c.start()
        sent.append((d, c))
    rows = GRID

    def mods(m):
        return [mod_ref[l, m : m + 1, :] for l in range(2)]

    def both(rows_of):
        return jnp.concatenate([rows_of(0), rows_of(1)], axis=0)

    def modulated(stream, o):
        shift, scale = mods(o), mods(o + 1)
        normed = layer_norm(stream)
        return both(
            lambda l: (normed[l * rows : (l + 1) * rows] * (1.0 + scale[l]) + shift[l]).astype(BF16)
        )

    def gated(stream, o, value):
        gate = mods(o)
        return both(
            lambda l: stream[l * rows : (l + 1) * rows] + gate[l] * value[l * rows : (l + 1) * rows]
        )

    stream_ref[...] = (
        jnp.dot(latb_ref[...], pw_ref[...], preferred_element_type=F32)
        + jnp.concatenate([pos_ref[...], pos_ref[...]], axis=0)
    )
    total = part_ref[me].astype(F32)
    for d, c in reversed(sent):
        c.wait()
        total = total + r1[d].astype(F32)
    stream = gated(stream_ref[...], 2, total + ob_ref[...])
    stream_ref[...] = stream
    gathered[me] = modulated(stream, 3)

    right, left = {"tp": (me + 1) % n}, {"tp": (me + n - 1) % n}

    def hop(k):
        held_r, held_l = (me - (k - 1) + n) % n, (me + (k - 1)) % n
        out = [remote(gathered.at[held_r], gathered.at[held_r], sr.at[k], qr.at[k], right)]
        if k < n // 2:
            out.append(remote(gathered.at[held_l], gathered.at[held_l], sl.at[k], ql.at[k], left))
        for c in out:
            c.start()
        return out

    def units(x):
        pre = jnp.dot(x, up_ref[...], preferred_element_type=F32) + upb_ref[...]
        hid = jax.nn.gelu(pre, approximate=True).astype(BF16)
        return jnp.dot(hid, down_ref[...], preferred_element_type=F32).astype(BF16)

    flying = []

    def give(k, value):
        held[k] = value
        peer = (me - k + n) % n
        c = remote(held.at[k], r2.at[k], s2.at[k], q2.at[k], {"tp": peer})
        c.start()
        flying.append((k, c))

    hops = hop(1)
    own[...] = units(gathered[me])
    for k in range(1, n // 2 + 1):
        for c in hops:
            c.wait()
        if k < n // 2:
            hops = hop(k + 1)
            x = jnp.concatenate([gathered[(me - k + n) % n], gathered[(me + k) % n]], axis=0)
            y = units(x)
            give(k, y[: 2 * rows])
            give(n - k, y[2 * rows :])
        else:
            give(k, units(gathered[(me - k + n) % n]))

    total = own[...].astype(F32)
    for k, c in flying:
        c.wait()
        total = total + r2[k].astype(F32)
    stream = gated(stream_ref[...], 5, total + downb_ref[...])
    value = jnp.dot(modulated(stream, 6), fw_ref[...], preferred_element_type=F32) + fb_ref[...]
    noise[...] = value
    c = remote(noise, other, s3, q3, {"cfg": 1 - half})
    c.start()
    c.wait()
    theirs = other[...]
    first = half == 0
    conditional = jnp.where(first, value, theirs)
    unconditional = jnp.where(first, theirs, value)
    guided = unconditional + GUIDANCE * (conditional - unconditional)
    out_ref[...] = c0_ref[...] * lat_ref[...] + c1_ref[...] * guided


def feed(n, *operands):
    vmem = pl.BlockSpec(memory_space=pltpu.VMEM)
    dma = pltpu.SemaphoreType.DMA
    rows = 2 * GRID
    return pl.pallas_call(
        functools.partial(feed_kernel, n),
        out_shape=jax.ShapeDtypeStruct((rows, LANES), F32),
        in_specs=[vmem] * len(operands),
        out_specs=vmem,
        scratch_shapes=[
            pltpu.VMEM((n, rows, D), BF16),
            pltpu.VMEM((n, rows, D), BF16),
            pltpu.VMEM((n, rows, D), BF16),
            pltpu.VMEM((n, rows, D), BF16),
            pltpu.VMEM((rows, D), F32),
            pltpu.VMEM((rows, D), BF16),
            pltpu.VMEM((rows, LANES), F32),
            pltpu.VMEM((rows, LANES), F32),
        ] + [dma((n,))] * 8 + [dma(()), dma(())],
        compiler_params=pltpu.CompilerParams(
            collective_id=1, has_side_effects=True, vmem_limit_bytes=60000000
        ),
        name="feed",
    )(*operands)


def pad_heads(value):
    split = value.reshape(value.shape[:-1] + (2, HEAD_DIM))
    wide = jnp.pad(split, [(0, 0)] * (split.ndim - 1) + [(0, LANES - HEAD_DIM)])
    return wide.reshape(value.shape[:-1] + (2 * LANES,))


def per_device(
    latents, timesteps, labels, solver_table, time_table, label_table, patch_weight, patch_bias,
    modulation_weight, modulation_bias, heads_weight, heads_bias, output_weight, output_bias,
    up_weight, up_bias, down_weight, down_bias, final_weight, final_bias,
):
    tp_n, rs_n = lax.axis_size("tp"), lax.axis_size("rs")
    tp, half, rs = lax.axis_index("tp"), lax.axis_index("cfg"), lax.axis_index("rs")
    group, quarter = rs // 4, rs % 4
    classes = label_table.shape[0] - 1
    local, latents_dev, patch = latents.shape
    share = local // tp_n

    class_ids = jnp.where(half == 0, labels.reshape(-1), classes)
    step_onehot = jax.nn.one_hot(timesteps.reshape(-1), time_table.shape[0], dtype=BF16)
    class_onehot = jax.nn.one_hot(class_ids, classes + 1, dtype=BF16)
    cond = jnp.dot(step_onehot, time_table, preferred_element_type=F32) + jnp.dot(
        class_onehot, label_table, preferred_element_type=F32
    )
    mine = D // tp_n
    cond = jnp.pad(cond, ((0, 0), (0, 2 * LANES - mine)))
    mrows = modulation_weight.shape[0]
    mw = jnp.transpose(modulation_weight.reshape(mrows, tp_n, mine), (1, 0, 2))
    mw = jnp.pad(mw, ((0, 0), (0, LANES - mrows), (0, 2 * LANES - mine)))
    mb = jnp.pad(modulation_bias, (0, LANES - mrows)).reshape(1, LANES)
    lat_t = jnp.transpose(latents.astype(BF16), (1, 2, 0)).reshape(latents_dev * patch, local)
    mod, lat_all = conditioning(cond, mw, mb, lat_t, tp_n, rs_n)
    width = mrows * tp_n
    mod = mod[:, :, :width].reshape(8, rs_n // 8, 2, width)
    mod = jnp.transpose(mod, (2, 0, 1, 3)).reshape(2, 8, D)

    row_np, col_np = position_tables()
    row_table = jnp.asarray(row_np)
    col_bias = jnp.asarray(col_np) + patch_bias[None, :]
    slots = (quarter + 4 - jnp.arange(4)) % 4
    row_slots = jnp.take(row_table.reshape(4, 8, D), slots, axis=0)
    lat_all = jnp.transpose(
        lat_all.reshape(4, latents_dev, patch, local), (1, 0, 3, 2)
    ).reshape(latents_dev, 4 * local, patch)

    hw, hb = heads_weight[0], heads_bias[0]
    wq = pad_heads(hw[:, 0])
    wkv = jnp.concatenate([pad_heads(hw[:, 1]), pad_heads(hw[:, 2])], axis=1)
    bq = pad_heads(hb[0]).reshape(1, -1)
    bkv = jnp.concatenate([pad_heads(hb[1]), pad_heads(hb[2])]).reshape(1, -1)
    wo = jnp.pad(
        output_weight[0].reshape(2, HEAD_DIM, D), ((0, 0), (0, LANES - HEAD_DIM), (0, 0))
    )
    partial = attention(
        lat_all, patch_weight, col_bias, row_slots, mod, wq, wkv, bq, bkv, wo
    ).reshape(8, 2 * GRID, D)

    own = lax.dynamic_slice_in_dim(latents, tp * share, share, 0)
    own = jnp.transpose(own, (1, 0, 2)).reshape(2 * share, patch)
    pos = col_bias + lax.dynamic_slice_in_dim(row_table, quarter * 8 + tp, 1, 0)
    step_own = lax.dynamic_index_in_dim(timesteps, group, 0, keepdims=False)
    hot = jax.nn.one_hot(step_own, solver_table.shape[0], dtype=F32)
    coef = jnp.dot(hot, solver_table, precision=lax.Precision.HIGHEST)
    coef = jnp.repeat(coef, share, axis=0)
    out = feed(
        tp_n, partial, jnp.pad(own, ((0, 0), (0, LANES - patch))), own.astype(BF16), patch_weight,
        pos, mod, output_bias, up_weight[0], up_bias, down_weight[0], down_bias,
        jnp.pad(final_weight, ((0, 0), (0, LANES - patch))),
        jnp.pad(final_bias, (0, LANES - patch)).reshape(1, LANES), coef[:, 0:1], coef[:, 1:2],
    )
    kept = lax.dynamic_slice_in_dim(out[:, :patch], half * (patch // 2), patch // 2, 1)
    return jnp.transpose(kept.reshape(latents_dev, share, patch // 2), (1, 0, 2))


def solution(mesh):
    in_specs = (
        P("rs", None, None), P(), P(), P(), P(None, "tp"), P(None, "tp"), P(), P(),
        P(("rs", "tp"), None), P(("rs", "tp")), P(None, None, None, "tp"), P(None, None, "tp"),
        P(None, "tp", None), P(), P(None, None, "tp"), P(None, "tp"), P(None, "tp", None), P(),
        P(), P(),
    )
    return jax.shard_map(
        per_device, mesh=mesh, in_specs=in_specs,
        out_specs=P(("rs", "tp"), None, "cfg"), check_vma=False,
    )
```

time: 999 us -> 160 us (0.16)
  the two profiles are of different devices: /device:TPU:4 before, /device:TPU:16 now
where the time goes in v1:
time: 160 us; the launch traced here: 159 us
  Pallas kernels  131 us (82%)
  local copies, waits for them, and re-layouts  21.9 us (14%)
  other arithmetic  5.34 us (3%)
    pallas_call x1, Pallas kernels, feed(): pl.pallas_call(functools.partial(feed_kernel, n), out_shape=jax.ShapeDtyp...  83.9 us
    pallas_call x1, Pallas kernels, conditioning(): pl.pallas_call(functools.partial(conditioning_kernel, tp_n, rs_n), out_sh...  32.1 us
    pallas_call x1, Pallas kernels, attention(): pl.pallas_call(attention_kernel, out_shape=jax.ShapeDtypeStruct((8, 2, GR...  15.5 us

profile of v1, /device:TPU:16, one launch (start us, length us, event | category | flops | bytes accessed | tf_op | source)
XLA Modules:
  0.0 159.4 jit_solution(14483349193770827476)
XLA Ops:
  0.0 0.9 dynamic-slice_reduce_fusion
  0.9 1.6 %broadcast_add_fusion = (f32[32,1152]{1,0:T(8,128)}, f32[32,1152]{1,0:T(8,128)}) fusion(f32[1152]{0:T(1024)S(1)} %dynamic-slice_reduce_fusion, f32[32,1152]{1,0:T(8,128)} %constant.88.clone, f32[1152]{0:T(1024)} %param.29), kind=kLoop, calls=%fused_computation.8 | loop fusion | flops 73728 | bytes 451584 | tf_op jit(solution)/shard_map/add | solution.py:386
  2.6 1.5 gather_fusion
  4.1 0.7 broadcast_select_fusion.row_ref
  4.9 0.7 copy.42
  5.6 0.7 pad.52
  6.3 0.7 copy.43
  7.0 0.7 pad.53
  7.9 1.1 pad_maximum_fusion.wkv_ref
  11.5 0.9 pad.49.w_ref
  13.5 32.1 %conditioning.1 = (f32[32,2,384]{2,1,0:T(2,128)}, bf16[4,32,256]{2,1,0:T(8,128)(2,1)}) custom-call(f32[16,256]{1,0:T(8,128)} %pad.48.cond_ref, bf16[8,128,256]{2,1,0:T(8,128)(2,1)} %pad.49.w_ref, f32[1,128]{1,0:T(1,128)} %pad_bitcast_fusion.3.b_ref, bf16[32,256]{1,0:T(8,128)(2,1)} %bitcast.77), custom_call_target="tpu_custom_call" | custom-call | tf_op jit(solution)/shard_map/conditioning/pallas_call | solution.py:110
  45.6 0.9 copy.66
  46.5 0.7 reshape.139.mod_ref
  47.2 1.8 %copy.39 = bf16[4,2,16,256]{2,3,0,1:T(8,128)(2,1)} copy(bf16[4,2,16,256]{3,2,1,0:T(8,128)(2,1)} %bitcast.76) | data formatting | bytes 131072 | tf_op jit(solution)/shard_map/reshape | solution.py:369
  49.1 0.7 copy.41
  49.8 0.7 pad.51
  50.5 0.9 copy.64
  52.0 0.9 pad.57.wo_ref
  52.9 15.5 %attention.1 = bf16[8,2,32,1152]{3,2,1,0:T(8,128)(2,1)} custom-call(bf16[2,1024,16]{2,1,0:T(8,128)(2,1)} %bitcast.62, bf16[16,1152]{1,0:T(8,128)(2,1)} %pw_ref.3, f32[32,1152]{1,0:T(8,128)} %get-tuple-element.16.col_ref, f32[4,8,1152]{2,1,0:T(8,128)} %broadcast_select_fusion.row_ref, f32[2,8,1152]{2,1,0:T(8,128)} %reshape.139.mod_ref, ...), custom_call_target="tpu_custom_call" | custom-call | tf_op jit(solution)/shard_map/attention/pallas_call | solution.py:181
  68.8 0.7 fusion.11
  70.8 1.7 %copy.45 = bf16[1,1152,576]{2,1,0:T(8,128)(2,1)} copy(bf16[1,1152,576]{1,2,0:T(8,128)(2,1)S(1)} %copy-done.1) | data formatting | bytes 2654208 | tf_op args[14]
  72.7 0.8 pad.59.fw_ref
  74.0 83.9 %feed.1 = f32[64,128]{1,0:T(8,128)} custom-call(bf16[8,64,1152]{2,1,0:T(8,128)(2,1)} %bitcast.57, f32[64,128]{1,0:T(8,128)} %pad.58.lat_ref, bf16[64,16]{1,0:T(8,128)(2,1)} %bitcast_convert_fusion.latb_ref, bf16[16,1152]{1,0:T(8,128)(2,1)} %pw_ref.3, f32[32,1152]{1,0:T(8,128)} %get-tuple-element.15.pos_ref, f32[2,8,1152]{2,1,0:T(8,128)} %reshape.139.mod_ref, ...), custom_call_target="tpu_custom_call" | custom-call | tf_op jit(solution)/shard_map/feed/pallas_call | solution.py:305
  157.9 0.8 constant_dynamic-slice_fusion
  (63 shorter events, 7.7 us)
Async XLA Ops:
  0.0 10.4 %copy-start = (bf16[1001,144]{0,1:T(8,128)(2,1)S(1)}, bf16[1001,144]{0,1:T(8,128)(2,1)}, u32[]{:S(2)}) copy-start(bf16[1001,144]{0,1:T(8,128)(2,1)} %param.27) | copy-start | bytes 864868
  0.0 4.8 %copy-start.2 = (bf16[1,1152,3,144]{1,3,2,0:T(8,128)(2,1)S(1)}, bf16[1,1152,3,144]{1,3,2,0:T(8,128)(2,1)}, u32[]{:S(2)}) copy-start(bf16[1,1152,3,144]{1,3,2,0:T(8,128)(2,1)} %param.32) | copy-start | bytes 2985988
  7.9 1.2 copy-start.8
  7.9 2.0 %copy-start.9 = (s32[8,2]{0,1:T(2,128)S(1)}, s32[8,2]{0,1:T(2,128)}, u32[]{:S(2)}) copy-start(s32[8,2]{0,1:T(2,128)} %param.24) | copy-start | bytes 196
  7.9 2.1 %copy-start.7 = (s32[8,2]{0,1:T(2,128)S(1)}, s32[8,2]{0,1:T(2,128)}, u32[]{:S(2)}) copy-start(s32[8,2]{0,1:T(2,128)} %param.23) | copy-start | bytes 196
  7.9 2.3 %copy-start.10 = (bf16[250,144]{0,1:T(8,128)(2,1)S(1)}, bf16[250,144]{0,1:T(8,128)(2,1)}, u32[]{:S(2)}) copy-start(bf16[250,144]{0,1:T(8,128)(2,1)} %param.26) | copy-start | bytes 216004
  7.9 3.3 %copy-start.4 = (bf16[36,1152]{1,0:T(8,128)(2,1)S(1)}, bf16[36,1152]{1,0:T(8,128)(2,1)}, u32[]{:S(2)}) copy-start(bf16[36,1152]{1,0:T(8,128)(2,1)} %param.30) | copy-start | bytes 248836
  9.1 3.3 %copy-start.5 = (f32[256,2,16]{0,2,1:T(8,128)S(1)}, f32[256,2,16]{0,2,1:T(8,128)}, u32[]{:S(2)}) copy-start(f32[256,2,16]{0,2,1:T(8,128)} %param.22) | copy-start | bytes 98308
  9.1 3.9 %copy-start.12 = (f32[36]{0:T(128)S(1)}, f32[36]{0:T(128)}, u32[]{:S(2)}) copy-start(f32[36]{0:T(128)} %param.31) | copy-start | bytes 436
  49.8 2.3 %copy-start.3 = (bf16[1,144,1152]{2,1,0:T(8,128)(2,1)S(1)}, bf16[1,144,1152]{2,1,0:T(8,128)(2,1)}, u32[]{:S(2)}) copy-start(bf16[1,144,1152]{2,1,0:T(8,128)(2,1)} %param.34) | copy-start | bytes 995332
  52.9 15.7 %copy-start.11 = (f32[250,2]{0,1:T(2,128)S(1)}, f32[250,2]{0,1:T(2,128)}, u32[]{:S(2)}) copy-start(f32[250,2]{0,1:T(2,128)} %param.25) | copy-start | bytes 6004
  52.9 17.9 %copy-start.1 = (bf16[1,1152,576]{1,2,0:T(8,128)(2,1)S(1)}, bf16[1,1152,576]{1,2,0:T(8,128)(2,1)}, u32[]{:S(2)}) copy-start(bf16[1,1152,576]{1,2,0:T(8,128)(2,1)} %param.36) | copy-start | bytes 3981316
  70.8 1.7 %copy-start.6 = (bf16[1152,16]{0,1:T(8,128)(2,1)S(1)}, bf16[1152,16]{0,1:T(8,128)(2,1)}, u32[]{:S(2)}) copy-start(bf16[1152,16]{0,1:T(8,128)(2,1)} %param.40) | copy-start | bytes 110596
  70.8 2.7 %copy-start.13 = (f32[16]{0:T(128)S(1)}, f32[16]{0:T(128)}, u32[]{:S(2)}) copy-start(f32[16]{0:T(128)} %param.41) | copy-start | bytes 196

commit v2 on v1

v2 whole, which is shorter than its diff:
```python
import functools

import jax
import jax.numpy as jnp
import numpy as np
from jax import lax
from jax.experimental import pallas as pl
from jax.experimental.pallas import tpu as pltpu
from jax.sharding import PartitionSpec as P

HEAD_DIM = 72
GRID = 32
D = 1152
LANES = 128
GUIDANCE = 4.0
MESH = pl.DeviceIdType.MESH
F32, BF16 = jnp.float32, jnp.bfloat16


def remote(src, dst, send, recv, device):
    return pltpu.make_async_remote_copy(
        src_ref=src, dst_ref=dst, send_sem=send, recv_sem=recv, device_id=device, device_id_type=MESH
    )


def layer_norm(values):
    centre = values - jnp.mean(values, axis=-1, keepdims=True)
    spread = jnp.mean(centre * centre, axis=-1, keepdims=True)
    return centre * lax.rsqrt(spread + 1e-06)


def position_tables():
    count = D // 4
    frequency = 1.0 / 10000.0 ** (np.arange(count, dtype=np.float64) / count)
    angle = np.arange(GRID, dtype=np.float64)[:, None] * frequency[None, :]
    half = np.concatenate([np.sin(angle), np.cos(angle)], axis=1)
    zero = np.zeros_like(half)
    row = np.concatenate([half, zero], axis=1).astype(np.float32)
    col = np.concatenate([zero, half], axis=1).astype(np.float32)
    return row, col


def conditioning_kernel(
    tp_n, rs_n, cond_ref, w_ref, b_ref, lat_ref, out_ref, latall_ref,
    cbuf, part, pbuf, blk, gbuf, obuf, lbuf, s1, r1, s2, r2, s3, r3, s4, r4, s5, r5,
):
    tp, rs = lax.axis_index("tp"), lax.axis_index("rs")
    quarter, group, groups = rs % 4, rs // 4, rs_n // 4
    barrier = pltpu.get_barrier_semaphore()

    def at_tp(d):
        return {"tp": (tp + d) % tp_n}

    def at_quarter(d):
        return {"rs": group * 4 + (quarter + d) % 4}

    def at_group(d):
        return {"rs": ((group + d) % groups) * 4 + quarter}

    for d in range(1, tp_n):
        pl.semaphore_signal(barrier, inc=1, device_id=at_tp(d), device_id_type=MESH)
    for d in range(1, groups):
        pl.semaphore_signal(barrier, inc=1, device_id=at_group(d), device_id_type=MESH)
    for d in range(1, 4):
        pl.semaphore_signal(barrier, inc=1, device_id=at_quarter(d), device_id_type=MESH)
    pl.semaphore_wait(barrier, tp_n - 1 + groups - 1 + 3)

    first = []
    for d in range(1, tp_n):
        c = remote(cond_ref, cbuf.at[tp], s1.at[d], r1.at[d], at_tp(d))
        c.start()
        first.append(c)
    lats = []
    for d in range(1, 4):
        c = remote(lat_ref, lbuf.at[d], s4.at[d], r4.at[d], at_quarter(d))
        c.start()
        lats.append(c)
    cbuf[tp] = cond_ref[...]
    latall_ref[0] = lat_ref[...]
    for c in first:
        c.wait()
    total = jnp.broadcast_to(b_ref[...], (cond_ref.shape[0], LANES))
    for t in range(tp_n):
        v = cbuf[t]
        act = (v / (1.0 + jnp.exp(-v))).astype(BF16)
        total = total + lax.dot_general(
            act, w_ref[t], (((1,), (1,)), ((), ())), preferred_element_type=F32
        )
    part[...] = total
    second = []
    for d in range(1, tp_n):
        c = remote(part, pbuf.at[tp], s2.at[d], r2.at[d], at_tp(d))
        c.start()
        second.append(c)
    pbuf[tp] = total
    for d in range(1, 4):
        lats[d - 1].wait()
        latall_ref[d] = lbuf[d]
    for c in second:
        c.wait()
    share = D * 8 // (tp_n * rs_n)
    rows = jnp.concatenate([pbuf[t][:, :share] for t in range(tp_n)], axis=1)
    width = rows.shape[1]
    rows = jnp.concatenate([rows, jnp.zeros((rows.shape[0], 3 * LANES - width), F32)], axis=1)
    for g in range(groups):
        blk[g] = rows[2 * g : 2 * g + 2, :]
    third = []
    for d in range(1, groups):
        c = remote(blk.at[(group + d) % groups], gbuf.at[group], s3.at[d], r3.at[d], at_group(d))
        c.start()
        third.append(c)
    gbuf[group] = blk[group]
    for c in third:
        c.wait()
    fourth = []
    for d in range(1, 4):
        c = remote(gbuf, obuf.at[quarter], s5.at[d], r5.at[d], at_quarter(d))
        c.start()
        fourth.append(c)
    obuf[quarter] = gbuf[...]
    for c in fourth:
        c.wait()
    for l in range(2):
        out_ref[l] = jnp.concatenate([obuf[q, :, l, :][:, :width] for q in range(4)], axis=1)


def conditioning(cond, weight, bias, lat, tp_n, rs_n):
    n = cond.shape[0]
    wide, groups = 3 * LANES, rs_n // 4
    vmem = pl.BlockSpec(memory_space=pltpu.VMEM)
    dma = pltpu.SemaphoreType.DMA
    return pl.pallas_call(
        functools.partial(conditioning_kernel, tp_n, rs_n),
        out_shape=(
            jax.ShapeDtypeStruct((2, groups, D), F32),
            jax.ShapeDtypeStruct((4,) + lat.shape, BF16),
        ),
        in_specs=[vmem] * 4,
        out_specs=(vmem, vmem),
        scratch_shapes=[
            pltpu.VMEM((tp_n,) + cond.shape, F32),
            pltpu.VMEM((n, LANES), F32),
            pltpu.VMEM((tp_n, n, LANES), F32),
            pltpu.VMEM((groups, 2, wide), F32),
            pltpu.VMEM((groups, 2, wide), F32),
            pltpu.VMEM((4, groups, 2, wide), F32),
            pltpu.VMEM((4,) + lat.shape, BF16),
            dma((tp_n,)), dma((tp_n,)), dma((tp_n,)), dma((tp_n,)),
            dma((groups,)), dma((groups,)), dma((4,)), dma((4,)), dma((4,)), dma((4,)),
        ],
        compiler_params=pltpu.CompilerParams(collective_id=0, has_side_effects=True),
        name="conditioning",
    )(cond, weight, bias, lat)


def attention_kernel(lat_ref, pw_ref, pb_ref, col_ref, row_ref, mod_ref, w_ref, b_ref,
                     wo_ref, out_ref, normed, kv):
    tile, wide = 256, 2 * LANES
    quarter = lax.axis_index("rs") % 4

    def fill(latent, slot):
        emb = lax.dot_general(
            lat_ref[slot, latent], pw_ref[...], (((0,), (0,)), ((), ())),
            preferred_element_type=F32,
        )
        shift, scale = mod_ref[latent, 0:1, :], 1.0 + mod_ref[latent, 1:2, :]
        col = col_ref[...] + pb_ref[...]
        place = pl.multiple_of(((quarter + 4 - slot) % 4) * 8, 8)
        row = row_ref[pl.ds(place, 8), :]
        for i in range(tile // GRID):
            stream = (emb[i * GRID : (i + 1) * GRID] + col) + row[i : i + 1, :]
            normed[i * GRID : (i + 1) * GRID, :] = (
                layer_norm(stream) * scale + shift
            ).astype(BF16)
        pair = jnp.dot(normed[...], w_ref[:, wide:], preferred_element_type=F32) + b_ref[:, wide:]
        kv[pl.ds(pl.multiple_of(slot * tile, tile), tile), :] = pair.astype(BF16)

    @pl.loop(0, 2)
    def _(latent):
        @pl.loop(0, 4)
        def _(step):
            fill(latent, 3 - step)

        queries = (
            jnp.dot(normed[...], w_ref[:, :wide], preferred_element_type=F32) + b_ref[:, :wide]
        )
        lane = lax.broadcasted_iota(jnp.int32, (tile, wide), 1)
        heads = []
        for h in range(2):
            inside = (lane >= h * HEAD_DIM) & (lane < (h + 1) * HEAD_DIM)
            q = jnp.where(inside, queries, 0.0).astype(BF16)
            scores = lax.dot_general(
                q, kv[:, :wide], (((1,), (1,)), ((), ())), preferred_element_type=F32
            ) * HEAD_DIM ** (-0.5)
            exponent = jnp.exp(scores - jnp.max(scores, axis=-1, keepdims=True))
            row_total = jnp.sum(exponent, axis=-1, keepdims=True)
            weighted = jnp.dot(exponent.astype(BF16), kv[:, wide:], preferred_element_type=F32)
            heads.append(weighted / row_total)
        attended = jnp.where(lane < HEAD_DIM, heads[0], heads[1]).astype(BF16)
        result = jnp.dot(
            attended[:, : 2 * HEAD_DIM], wo_ref[...], preferred_element_type=F32
        ).astype(BF16)
        for t in range(8):
            out_ref[t, latent] = result[t * GRID : (t + 1) * GRID, :]


def attention(*operands):
    vmem = pl.BlockSpec(memory_space=pltpu.VMEM)
    return pl.pallas_call(
        attention_kernel,
        out_shape=jax.ShapeDtypeStruct((8, 2, GRID, D), BF16),
        in_specs=[vmem] * len(operands),
        out_specs=vmem,
        scratch_shapes=[pltpu.VMEM((256, D), BF16), pltpu.VMEM((1024, 4 * LANES), BF16)],
        compiler_params=pltpu.CompilerParams(vmem_limit_bytes=60000000),
        name="attention",
    )(*operands)


def feed_kernel(
    n, part_ref, lat_ref, pw_ref, pb_ref, col_ref, row_ref, mod_ref, ob_ref, up_ref, upb_ref,
    down_ref, downb_ref, fw_ref, fb_ref, c0_ref, c1_ref, out_ref,
    chain, gathered, held, r2, stream_ref, own, noise, other,
    s1, q1, sr, qr, sl, ql, s2, q2, s3, q3,
):
    me, half = lax.axis_index("tp"), lax.axis_index("cfg")
    barrier = pltpu.get_barrier_semaphore()
    for d in range(1, n):
        pl.semaphore_signal(barrier, inc=1, device_id={"tp": (me + d) % n}, device_id_type=MESH)
    pl.semaphore_signal(barrier, inc=1, device_id={"cfg": 1 - half}, device_id_type=MESH)
    pl.semaphore_wait(barrier, n)

    right, left = {"tp": (me + 1) % n}, {"tp": (me + n - 1) % n}
    hops_of = (n // 2, n // 2 - 1)

    def owner(side, k):
        return (me + n // 2 - (k - 1)) % n if side == 0 else (me - hops_of[1] + (k - 1) + n) % n

    def link(side, k, l):
        i = (side * 2 + l) * 8 + k
        src = part_ref.at[owner(side, 1), l] if k == 1 else chain.at[0, i]
        return remote(src, chain.at[1, i], s1.at[i], q1.at[i], left if side else right)

    chained = {}
    for l in range(2):
        for side in range(2):
            chained[side, 1, l] = link(side, 1, l)
            chained[side, 1, l].start()
    rows = GRID

    def mods(m):
        return [mod_ref[l, m : m + 1, :] for l in range(2)]

    def both(rows_of):
        return jnp.concatenate([rows_of(0), rows_of(1)], axis=0)

    def modulated(stream, o):
        shift, scale = mods(o), mods(o + 1)
        normed = layer_norm(stream)
        return both(
            lambda l: (normed[l * rows : (l + 1) * rows] * (1.0 + scale[l]) + shift[l]).astype(BF16)
        )

    def gated(stream, o, value):
        gate = mods(o)
        return both(
            lambda l: stream[l * rows : (l + 1) * rows] + gate[l] * value[l * rows : (l + 1) * rows]
        )

    row = row_ref[pl.ds((lax.axis_index("rs") % 4) * 8 + me, 1), :]
    place = (col_ref[...] + pb_ref[...]) + row
    stream_ref[...] = jnp.dot(
        lat_ref[...].astype(BF16), pw_ref[...], preferred_element_type=F32
    ) + jnp.concatenate([place, place], axis=0)
    for k in range(2, n // 2 + 1):
        for l in range(2):
            for side in range(2):
                if k <= hops_of[side]:
                    i = (side * 2 + l) * 8 + k
                    chained[side, k - 1, l].wait_recv()
                    chain[0, i] = (
                        chain[1, i - 1].astype(F32) + part_ref[owner(side, k), l].astype(F32)
                    ).astype(BF16)
                    chained[side, k, l] = link(side, k, l)
                    chained[side, k, l].start()
    sums = []
    for l in range(2):
        total = part_ref[me, l].astype(F32)
        for side in (1, 0):
            k = hops_of[side]
            chained[side, k, l].wait_recv()
            total = total + chain[1, (side * 2 + l) * 8 + k].astype(F32)
        sums.append(total)
    total = jnp.concatenate(sums, axis=0)
    stream = gated(stream_ref[...], 2, total + ob_ref[...])
    stream_ref[...] = stream
    gathered[me] = modulated(stream, 3)

    def hop(k):
        held_r, held_l = (me - (k - 1) + n) % n, (me + (k - 1)) % n
        out = [remote(gathered.at[held_r], gathered.at[held_r], sr.at[k], qr.at[k], right)]
        if k < n // 2:
            out.append(remote(gathered.at[held_l], gathered.at[held_l], sl.at[k], ql.at[k], left))
        for c in out:
            c.start()
        return out

    def units(x):
        pre = jnp.dot(x, up_ref[...], preferred_element_type=F32) + upb_ref[...]
        hid = jax.nn.gelu(pre, approximate=True).astype(BF16)
        return jnp.dot(hid, down_ref[...], preferred_element_type=F32).astype(BF16)

    flying = []

    def give(k, value):
        held[k] = value
        peer = (me - k + n) % n
        c = remote(held.at[k], r2.at[k], s2.at[k], q2.at[k], {"tp": peer})
        c.start()
        flying.append((k, c))

    hops = hop(1)
    own[...] = units(gathered[me])
    for k in range(1, n // 2 + 1):
        for c in hops:
            c.wait()
        if k < n // 2:
            hops = hop(k + 1)
            x = jnp.concatenate([gathered[(me - k + n) % n], gathered[(me + k) % n]], axis=0)
            y = units(x)
            give(k, y[: 2 * rows])
            give(n - k, y[2 * rows :])
        else:
            give(k, units(gathered[(me - k + n) % n]))

    for c in chained.values():
        c.wait_send()
    total = own[...].astype(F32)
    for k, c in flying:
        c.wait()
        total = total + r2[k].astype(F32)
    stream = gated(stream_ref[...], 5, total + downb_ref[...])
    value = jnp.dot(modulated(stream, 6), fw_ref[...], preferred_element_type=F32) + fb_ref[...]
    noise[...] = value
    c = remote(noise, other, s3, q3, {"cfg": 1 - half})
    c.start()
    c.wait()
    theirs = other[...]
    first = half == 0
    conditional = jnp.where(first, value, theirs)
    unconditional = jnp.where(first, theirs, value)
    guided = unconditional + GUIDANCE * (conditional - unconditional)
    out_ref[...] = c0_ref[...] * lat_ref[...] + c1_ref[...] * guided


def feed(n, *operands):
    vmem = pl.BlockSpec(memory_space=pltpu.VMEM)
    dma = pltpu.SemaphoreType.DMA
    rows = 2 * GRID
    return pl.pallas_call(
        functools.partial(feed_kernel, n),
        out_shape=jax.ShapeDtypeStruct((rows, 16), F32),
        in_specs=[vmem] * len(operands),
        out_specs=vmem,
        scratch_shapes=[
            pltpu.VMEM((2, 32, GRID, D), BF16),
            pltpu.VMEM((n, rows, D), BF16),
            pltpu.VMEM((n, rows, D), BF16),
            pltpu.VMEM((n, rows, D), BF16),
            pltpu.VMEM((rows, D), F32),
            pltpu.VMEM((rows, D), BF16),
            pltpu.VMEM((rows, 16), F32),
            pltpu.VMEM((rows, 16), F32),
        ] + [dma((32,))] * 2 + [dma((n,))] * 6 + [dma(()), dma(())],
        compiler_params=pltpu.CompilerParams(
            collective_id=1, has_side_effects=True, vmem_limit_bytes=60000000
        ),
        name="feed",
    )(*operands)


def per_device(
    latents, timesteps, labels, solver_table, time_table, label_table, patch_weight, patch_bias,
    modulation_weight, modulation_bias, heads_weight, heads_bias, output_weight, output_bias,
    up_weight, up_bias, down_weight, down_bias, final_weight, final_bias,
):
    tp_n, rs_n = lax.axis_size("tp"), lax.axis_size("rs")
    tp, half, rs = lax.axis_index("tp"), lax.axis_index("cfg"), lax.axis_index("rs")
    group, quarter = rs // 4, rs % 4
    classes = label_table.shape[0] - 1
    local, latents_dev, patch = latents.shape
    share = local // tp_n

    class_ids = jnp.where(half == 0, labels.reshape(-1), classes)
    step_onehot = jax.nn.one_hot(timesteps.reshape(-1), time_table.shape[0], dtype=BF16)
    class_onehot = jax.nn.one_hot(class_ids, classes + 1, dtype=BF16)
    cond = jnp.dot(step_onehot, time_table, preferred_element_type=F32) + jnp.dot(
        class_onehot, label_table, preferred_element_type=F32
    )
    mine = D // tp_n
    cond = jnp.pad(cond, ((0, 0), (0, 2 * LANES - mine)))
    mrows = modulation_weight.shape[0]
    mw = jnp.transpose(modulation_weight.reshape(mrows, tp_n, mine), (1, 0, 2))
    mw = jnp.pad(mw, ((0, 0), (0, LANES - mrows), (0, 2 * LANES - mine)))
    mb = jnp.pad(modulation_bias, (0, LANES - mrows)).reshape(1, LANES)
    lat_t = jnp.transpose(latents.astype(BF16), (1, 2, 0))
    mod, lat_all = conditioning(cond, mw, mb, lat_t, tp_n, rs_n)

    row_np, col_np = position_tables()
    row, col = jnp.asarray(row_np), jnp.asarray(col_np)
    patch_bias = patch_bias.reshape(1, D)
    fill = 2 * LANES - mine
    w = jnp.pad(heads_weight[0], ((0, 0), (0, 0), (0, fill))).reshape(D, 6 * LANES)
    b = jnp.pad(heads_bias[0], ((0, 0), (0, fill))).reshape(1, 6 * LANES)
    partial = attention(lat_all, patch_weight, patch_bias, col, row, mod, w, b, output_weight[0])

    own = lax.dynamic_slice_in_dim(latents, tp * share, share, 0)
    own = jnp.transpose(own, (1, 0, 2)).reshape(2 * share, patch)
    step_own = lax.dynamic_index_in_dim(timesteps, group, 0, keepdims=False)
    hot = jax.nn.one_hot(step_own, solver_table.shape[0], dtype=F32)
    coef = jnp.dot(hot, solver_table, precision=lax.Precision.HIGHEST)
    coef = jnp.repeat(coef, share, axis=0)
    out = feed(
        tp_n, partial, own, patch_weight, patch_bias, col, row, mod, output_bias, up_weight[0],
        up_bias, down_weight[0], down_bias, final_weight, final_bias.reshape(1, patch),
        coef[:, 0:1], coef[:, 1:2],
    )
    kept = lax.dynamic_slice_in_dim(out, half * (patch // 2), patch // 2, 1)
    return jnp.transpose(kept.reshape(latents_dev, share, patch // 2), (1, 0, 2))


def solution(mesh):
    in_specs = (
        P("rs", None, None), P(), P(), P(), P(None, "tp"), P(None, "tp"), P(), P(),
        P(("rs", "tp"), None), P(("rs", "tp")), P(None, None, None, "tp"), P(None, None, "tp"),
        P(None, "tp", None), P(), P(None, None, "tp"), P(None, "tp"), P(None, "tp", None), P(),
        P(), P(),
    )
    return jax.shard_map(
        per_device, mesh=mesh, in_specs=in_specs,
        out_specs=P(("rs", "tp"), None, "cfg"), check_vma=False,
    )
```

time: 160 us -> 139 us (0.87)
  the two profiles are of different devices: /device:TPU:16 before, /device:TPU:4 now
where the time goes in v2:
time: 139 us; the launch traced here: 138 us
  Pallas kernels  122 us (88%)
  local copies, waits for them, and re-layouts  13.6 us (10%)
  matrix products  1.44 us (1%)
    pallas_call x1, Pallas kernels, feed(): pl.pallas_call(functools.partial(feed_kernel, n), out_shape=jax.ShapeDtyp...  70.5 us
    pallas_call x1, Pallas kernels, conditioning(): pl.pallas_call(functools.partial(conditioning_kernel, tp_n, rs_n), out_sh...  35.5 us
    pallas_call x1, Pallas kernels, attention(): pl.pallas_call(attention_kernel, out_shape=jax.ShapeDtypeStruct((8, 2, GR...  15.8 us
    unnamed x26, local copies, waits for them, and re-layouts  4.03 us

profile of v2, /device:TPU:4, one launch (start us, length us, event | category | flops | bytes accessed | tf_op | source)
XLA Modules:
  0.0 138.2 jit_solution(11280086530067982536)
XLA Ops:
  0.0 0.9 copy.32
  1.0 1.0 fusion.1
  2.0 0.7 broadcast_select_fusion
  2.9 0.2 convolution_add_fusion
  3.1 0.6 pad.20.cond_ref
  3.7 1.1 reshape.41
  4.9 0.8 pad.21.w_ref
  5.7 0.5 pad_bitcast_fusion.1.b_ref
  6.2 0.6 convert_bitcast_fusion.lat_ref
  6.9 35.5 %conditioning.1 = (f32[2,8,1152]{2,1,0:T(8,128)}, bf16[4,2,16,256]{3,2,1,0:T(8,128)(2,1)}) custom-call(f32[16,256]{1,0:T(8,128)} %pad.20.cond_ref, bf16[8,128,256]{2,1,0:T(8,128)(2,1)} %pad.21.w_ref, f32[1,128]{1,0:T(1,128)} %pad_bitcast_fusion.1.b_ref, bf16[2,16,256]{2,1,0:T(8,128)(2,1)} %convert_bitcast_fusion.lat_ref), custom_call_target="tpu_custom_call" | custom-call | tf_op jit(solution)/shard_map/conditioning/pallas_call | solution.py:132
  42.4 0.6 reshape.43.pb_ref
  43.0 0.1 pad.23
  43.2 2.3 %copy.35.w_ref = bf16[1152,768]{1,0:T(8,128)(2,1)} copy(bf16[1152,768]{0,1:T(8,128)(2,1)S(1)} %bitcast.29) | data formatting | bytes 3538944 | tf_op jit(solution)/shard_map/reshape | solution.py:413
  45.4 0.6 copy.49
  46.0 15.8 %attention.1.part_ref = bf16[8,2,32,1152]{3,2,1,0:T(8,128)(2,1)} custom-call(bf16[4,2,16,256]{3,2,1,0:T(8,128)(2,1)} %get-tuple-element.7.lat_ref, bf16[16,1152]{1,0:T(8,128)(2,1)} %pw_ref.3, f32[1,1152]{1,0:T(1,128)} %reshape.43.pb_ref, f32[32,1152]{1,0:T(8,128)} %constant.55.clone.col_ref, f32[32,1152]{1,0:T(8,128)} %constant.54.clone.row_ref, ...), custom_call_target="tpu_custom_call" | custom-call | tf_op jit(solution)/shard_map/attention/pallas_call | solution.py:209
  61.9 0.7 copy.36
  62.6 1.7 %copy.37 = bf16[1,1152,576]{2,1,0:T(8,128)(2,1)} copy(bf16[1,1152,576]{1,2,0:T(8,128)(2,1)S(1)} %copy-done.1) | data formatting | bytes 2654208 | tf_op args[14]
  64.3 0.9 copy.41.fw_ref
  65.2 0.2 dynamic-slice_reduce_fusion
  65.4 0.2 fusion.3
  65.5 0.7 fusion.7
  66.2 70.5 %feed.1 = f32[64,16]{1,0:T(8,128)} custom-call(bf16[8,2,32,1152]{3,2,1,0:T(8,128)(2,1)} %attention.1.part_ref, f32[64,16]{1,0:T(8,128)} %bitcast.36, bf16[16,1152]{1,0:T(8,128)(2,1)} %pw_ref.3, f32[1,1152]{1,0:T(1,128)} %reshape.43.pb_ref, f32[32,1152]{1,0:T(8,128)} %constant.55.clone.col_ref, f32[32,1152]{1,0:T(8,128)} %constant.54.clone.row_ref, ...), custom_call_target="tpu_custom_call" | custom-call | tf_op jit(solution)/shard_map/feed/pallas_call | solution.py:360
  136.7 0.8 constant_dynamic-slice_fusion
  137.6 0.6 copy.43
  (29 shorter events, 0.5 us)
Async XLA Ops:
  0.0 2.9 %copy-start = (bf16[1001,144]{0,1:T(8,128)(2,1)S(1)}, bf16[1001,144]{0,1:T(8,128)(2,1)}, u32[]{:S(2)}) copy-start(bf16[1001,144]{0,1:T(8,128)(2,1)} %param.27) | copy-start | bytes 864868
  0.0 5.7 %copy-start.9 = (f32[36]{0:T(128)S(1)}, f32[36]{0:T(128)}, u32[]{:S(2)}) copy-start(f32[36]{0:T(128)} %param.31) | copy-start | bytes 436
  0.0 6.2 %copy-start.3 = (f32[256,2,16]{0,2,1:T(8,128)S(1)}, f32[256,2,16]{0,2,1:T(8,128)}, u32[]{:S(2)}) copy-start(f32[256,2,16]{0,2,1:T(8,128)} %param.22) | copy-start | bytes 98308
  0.0 42.4 %copy-start.5 = (f32[1152]{0:T(1024)S(1)}, f32[1152]{0:T(1024)}, u32[]{:S(2)}) copy-start(f32[1152]{0:T(1024)} %param.29) | copy-start | bytes 13828
  0.0 43.0 %copy-start.2 = (bf16[1,1152,3,144]{1,3,2,0:T(8,128)(2,1)S(1)}, bf16[1,1152,3,144]{1,3,2,0:T(8,128)(2,1)}, u32[]{:S(2)}) copy-start(bf16[1,1152,3,144]{1,3,2,0:T(8,128)(2,1)} %param.32) | copy-start | bytes 2985988
  43.1 2.3 %copy-start.7 = (f32[1,3,144]{2,0,1:T(1,128)S(1)}, f32[1,3,144]{2,0,1:T(1,128)}, u32[]{:S(2)}) copy-start(f32[1,3,144]{2,0,1:T(1,128)} %param.33) | copy-start | bytes 5188
  46.0 16.6 %copy-start.1 = (bf16[1,1152,576]{1,2,0:T(8,128)(2,1)S(1)}, bf16[1,1152,576]{1,2,0:T(8,128)(2,1)}, u32[]{:S(2)}) copy-start(bf16[1,1152,576]{1,2,0:T(8,128)(2,1)} %param.36) | copy-start | bytes 3981316
  61.8 2.4 %copy-start.4 = (bf16[1152,16]{0,1:T(8,128)(2,1)S(1)}, bf16[1152,16]{0,1:T(8,128)(2,1)}, u32[]{:S(2)}) copy-start(bf16[1152,16]{0,1:T(8,128)(2,1)} %param.40) | copy-start | bytes 110596
  62.6 2.5 %copy-start.6 = (s32[8,2]{0,1:T(2,128)S(1)}, s32[8,2]{0,1:T(2,128)}, u32[]{:S(2)}) copy-start(s32[8,2]{0,1:T(2,128)} %param.23) | copy-start | bytes 196
  62.6 2.7 %copy-start.8 = (f32[250,2]{0,1:T(2,128)S(1)}, f32[250,2]{0,1:T(2,128)}, u32[]{:S(2)}) copy-start(f32[250,2]{0,1:T(2,128)} %param.25) | copy-start | bytes 6004

commit v3 on v2

--- a/solution.py
+++ b/solution.py
@@ -79,13 +79,11 @@
     latall_ref[0] = lat_ref[...]
     for c in first:
         c.wait()
-    total = jnp.broadcast_to(b_ref[...], (cond_ref.shape[0], LANES))
-    for t in range(tp_n):
-        v = cbuf[t]
-        act = (v / (1.0 + jnp.exp(-v))).astype(BF16)
-        total = total + lax.dot_general(
-            act, w_ref[t], (((1,), (1,)), ((), ())), preferred_element_type=F32
-        )
+    v = jnp.concatenate([cbuf[t] for t in range(tp_n)], axis=1)
+    act = (v / (1.0 + jnp.exp(-v))).astype(BF16)
+    total = lax.dot_general(
+        act, w_ref[...], (((1,), (1,)), ((), ())), preferred_element_type=F32
+    ) + b_ref[...]
     part[...] = total
     second = []
     for d in range(1, tp_n):
@@ -98,8 +96,7 @@
         latall_ref[d] = lbuf[d]
     for c in second:
         c.wait()
-    share = D * 8 // (tp_n * rs_n)
-    rows = jnp.concatenate([pbuf[t][:, :share] for t in range(tp_n)], axis=1)
+    rows = jnp.concatenate([pbuf[t] for t in range(tp_n)], axis=1)
     width = rows.shape[1]
     rows = jnp.concatenate([rows, jnp.zeros((rows.shape[0], 3 * LANES - width), F32)], axis=1)
     for g in range(groups):
@@ -125,7 +122,7 @@
 
 
 def conditioning(cond, weight, bias, lat, tp_n, rs_n):
-    n = cond.shape[0]
+    n, share = cond.shape[0], weight.shape[0]
     wide, groups = 3 * LANES, rs_n // 4
     vmem = pl.BlockSpec(memory_space=pltpu.VMEM)
     dma = pltpu.SemaphoreType.DMA
@@ -139,8 +136,8 @@
         out_specs=(vmem, vmem),
         scratch_shapes=[
             pltpu.VMEM((tp_n,) + cond.shape, F32),
-            pltpu.VMEM((n, LANES), F32),
-            pltpu.VMEM((tp_n, n, LANES), F32),
+            pltpu.VMEM((n, share), F32),
+            pltpu.VMEM((tp_n, n, share), F32),
             pltpu.VMEM((groups, 2, wide), F32),
             pltpu.VMEM((groups, 2, wide), F32),
             pltpu.VMEM((4, groups, 2, wide), F32),
@@ -155,8 +152,13 @@
 
 def attention_kernel(lat_ref, pw_ref, pb_ref, col_ref, row_ref, mod_ref, w_ref, b_ref,
                      wo_ref, out_ref, normed, kv):
-    tile, wide = 256, 2 * LANES
+    tile, wide = 256, 2 * HEAD_DIM
     quarter = lax.axis_index("rs") % 4
+
+    def project(i):
+        return lax.dot_general(
+            normed[...], w_ref[i], (((1,), (1,)), ((), ())), preferred_element_type=F32
+        ) + b_ref[i : i + 1, :]
 
     def fill(latent, slot):
         emb = lax.dot_general(
@@ -172,8 +174,8 @@
             normed[i * GRID : (i + 1) * GRID, :] = (
                 layer_norm(stream) * scale + shift
             ).astype(BF16)
-        pair = jnp.dot(normed[...], w_ref[:, wide:], preferred_element_type=F32) + b_ref[:, wide:]
-        kv[pl.ds(pl.multiple_of(slot * tile, tile), tile), :] = pair.astype(BF16)
+        for i in range(2):
+            kv[i, pl.ds(pl.multiple_of(slot * tile, tile), tile), :] = project(i + 1).astype(BF16)
 
     @pl.loop(0, 2)
     def _(latent):
@@ -181,25 +183,21 @@
         def _(step):
             fill(latent, 3 - step)
 
-        queries = (
-            jnp.dot(normed[...], w_ref[:, :wide], preferred_element_type=F32) + b_ref[:, :wide]
-        )
+        queries = project(0)
         lane = lax.broadcasted_iota(jnp.int32, (tile, wide), 1)
         heads = []
         for h in range(2):
             inside = (lane >= h * HEAD_DIM) & (lane < (h + 1) * HEAD_DIM)
             q = jnp.where(inside, queries, 0.0).astype(BF16)
             scores = lax.dot_general(
-                q, kv[:, :wide], (((1,), (1,)), ((), ())), preferred_element_type=F32
+                q, kv[0], (((1,), (1,)), ((), ())), preferred_element_type=F32
             ) * HEAD_DIM ** (-0.5)
             exponent = jnp.exp(scores - jnp.max(scores, axis=-1, keepdims=True))
             row_total = jnp.sum(exponent, axis=-1, keepdims=True)
-            weighted = jnp.dot(exponent.astype(BF16), kv[:, wide:], preferred_element_type=F32)
+            weighted = jnp.dot(exponent.astype(BF16), kv[1], preferred_element_type=F32)
             heads.append(weighted / row_total)
         attended = jnp.where(lane < HEAD_DIM, heads[0], heads[1]).astype(BF16)
-        result = jnp.dot(
-            attended[:, : 2 * HEAD_DIM], wo_ref[...], preferred_element_type=F32
-        ).astype(BF16)
+        result = jnp.dot(attended, wo_ref[...], preferred_element_type=F32).astype(BF16)
         for t in range(8):
             out_ref[t, latent] = result[t * GRID : (t + 1) * GRID, :]
 
@@ -211,7 +209,7 @@
         out_shape=jax.ShapeDtypeStruct((8, 2, GRID, D), BF16),
         in_specs=[vmem] * len(operands),
         out_specs=vmem,
-        scratch_shapes=[pltpu.VMEM((256, D), BF16), pltpu.VMEM((1024, 4 * LANES), BF16)],
+        scratch_shapes=[pltpu.VMEM((256, D), BF16), pltpu.VMEM((2, 1024, 2 * HEAD_DIM), BF16)],
         compiler_params=pltpu.CompilerParams(vmem_limit_bytes=60000000),
         name="attention",
     )(*operands)
@@ -220,8 +218,8 @@
 def feed_kernel(
     n, part_ref, lat_ref, pw_ref, pb_ref, col_ref, row_ref, mod_ref, ob_ref, up_ref, upb_ref,
     down_ref, downb_ref, fw_ref, fb_ref, c0_ref, c1_ref, out_ref,
-    chain, gathered, held, r2, stream_ref, own, noise, other,
-    s1, q1, sr, qr, sl, ql, s2, q2, s3, q3,
+    chain, flight, gathered, held, stream_ref, noise, other,
+    s1, q1, sg, qg, s2, q2, s3, q3,
 ):
     me, half = lax.axis_index("tp"), lax.axis_index("cfg")
     barrier = pltpu.get_barrier_semaphore()
@@ -231,21 +229,49 @@
     pl.semaphore_wait(barrier, n)
 
     right, left = {"tp": (me + 1) % n}, {"tp": (me + n - 1) % n}
-    hops_of = (n // 2, n // 2 - 1)
-
-    def owner(side, k):
-        return (me + n // 2 - (k - 1)) % n if side == 0 else (me - hops_of[1] + (k - 1) + n) % n
-
-    def link(side, k, l):
+    far = n // 2
+
+    def hops_of(side, l):
+        return far if side == l else far - 1
+
+    def owner(side, l, k):
+        away = hops_of(side, l) - (k - 1)
+        return (me + away) % n if side == 0 else (me - away + n) % n
+
+    def chain_start(source, flight, sems, l, side):
+        i = (side * 2 + l) * 8 + 1
+        c = remote(source.at[owner(side, l, 1), l], flight.at[1, i], sems[0].at[i], sems[1].at[i],
+                   left if side else right)
+        c.start()
+        return c
+
+    def chain_step(source, flight, sems, chained, k, l, side):
         i = (side * 2 + l) * 8 + k
-        src = part_ref.at[owner(side, 1), l] if k == 1 else chain.at[0, i]
-        return remote(src, chain.at[1, i], s1.at[i], q1.at[i], left if side else right)
-
+        chained[side, k - 1, l].wait_recv()
+        flight[0, i] = (
+            flight[1, i - 1].astype(F32) + source[owner(side, l, k), l].astype(F32)
+        ).astype(BF16)
+        c = remote(flight.at[0, i], flight.at[1, i], sems[0].at[i], sems[1].at[i],
+                   left if side else right)
+        c.start()
+        chained[side, k, l] = c
+
+    def chain_end(source, flight, chained):
+        sums = []
+        for l in range(2):
+            total = source[me, l].astype(F32)
+            for side in range(2):
+                k = hops_of(side, l)
+                chained[side, k, l].wait_recv()
+                total = total + flight[1, (side * 2 + l) * 8 + k].astype(F32)
+            sums.append(total)
+        return jnp.concatenate(sums, axis=0)
+
+    one, two = (s1, q1), (s2, q2)
     chained = {}
     for l in range(2):
         for side in range(2):
-            chained[side, 1, l] = link(side, 1, l)
-            chained[side, 1, l].start()
+            chained[side, 1, l] = chain_start(part_ref, chain, one, l, side)
     rows = GRID
 
     def mods(m):
@@ -272,75 +298,69 @@
     stream_ref[...] = jnp.dot(
         lat_ref[...].astype(BF16), pw_ref[...], preferred_element_type=F32
     ) + jnp.concatenate([place, place], axis=0)
-    for k in range(2, n // 2 + 1):
+    for k in range(2, far + 1):
         for l in range(2):
             for side in range(2):
-                if k <= hops_of[side]:
-                    i = (side * 2 + l) * 8 + k
-                    chained[side, k - 1, l].wait_recv()
-                    chain[0, i] = (
-                        chain[1, i - 1].astype(F32) + part_ref[owner(side, k), l].astype(F32)
-                    ).astype(BF16)
-                    chained[side, k, l] = link(side, k, l)
-                    chained[side, k, l].start()
-    sums = []
-    for l in range(2):
-        total = part_ref[me, l].astype(F32)
-        for side in (1, 0):
-            k = hops_of[side]
-            chained[side, k, l].wait_recv()
-            total = total + chain[1, (side * 2 + l) * 8 + k].astype(F32)
-        sums.append(total)
-    total = jnp.concatenate(sums, axis=0)
+                if k <= hops_of(side, l):
+                    chain_step(part_ref, chain, one, chained, k, l, side)
+    total = chain_end(part_ref, chain, chained)
     stream = gated(stream_ref[...], 2, total + ob_ref[...])
     stream_ref[...] = stream
-    gathered[me] = modulated(stream, 3)
+    second = modulated(stream, 3)
+    gathered[me, 0], gathered[me, 1] = second[:rows], second[rows:]
 
     def hop(k):
-        held_r, held_l = (me - (k - 1) + n) % n, (me + (k - 1)) % n
-        out = [remote(gathered.at[held_r], gathered.at[held_r], sr.at[k], qr.at[k], right)]
-        if k < n // 2:
-            out.append(remote(gathered.at[held_l], gathered.at[held_l], sl.at[k], ql.at[k], left))
-        for c in out:
-            c.start()
+        out = []
+        for l in range(2):
+            for side in range(2):
+                if k <= hops_of(side, l):
+                    b = (me - (k - 1) + n) % n if side == 0 else (me + (k - 1)) % n
+                    i = (side * 2 + l) * 8 + k
+                    c = remote(gathered.at[b, l], gathered.at[b, l], sg.at[i], qg.at[i],
+                               left if side else right)
+                    c.start()
+                    out.append(c)
         return out
 
-    def units(x):
-        pre = jnp.dot(x, up_ref[...], preferred_element_type=F32) + upb_ref[...]
+    def units(blocks):
+        x = jnp.concatenate([gathered[b, l] for b in blocks for l in range(2)], axis=0)
+        pre = lax.dot_general(
+            x, up_ref[...], (((1,), (1,)), ((), ())), preferred_element_type=F32
+        ) + upb_ref[...]
         hid = jax.nn.gelu(pre, approximate=True).astype(BF16)
-        return jnp.dot(hid, down_ref[...], preferred_element_type=F32).astype(BF16)
-
-    flying = []
-
-    def give(k, value):
-        held[k] = value
-        peer = (me - k + n) % n
-        c = remote(held.at[k], r2.at[k], s2.at[k], q2.at[k], {"tp": peer})
-        c.start()
-        flying.append((k, c))
+        y = jnp.dot(hid, down_ref[...], preferred_element_type=F32).astype(BF16)
+        for j, b in enumerate(blocks):
+            for l in range(2):
+                held[b, l] = y[(2 * j + l) * rows : (2 * j + l + 1) * rows]
 
     hops = hop(1)
-    own[...] = units(gathered[me])
-    for k in range(1, n // 2 + 1):
+    units([me])
+    back = {}
+    for k in range(1, far):
         for c in hops:
             c.wait()
-        if k < n // 2:
-            hops = hop(k + 1)
-            x = jnp.concatenate([gathered[(me - k + n) % n], gathered[(me + k) % n]], axis=0)
-            y = units(x)
-            give(k, y[: 2 * rows])
-            give(n - k, y[2 * rows :])
-        else:
-            give(k, units(gathered[(me - k + n) % n]))
-
-    for c in chained.values():
+        hops = hop(k + 1)
+        units([(me - k + n) % n, (me + k) % n])
+    for l in range(2):
+        back[1 - l, 1, l] = chain_start(held, flight, two, l, 1 - l)
+    for c in hops:
+        c.wait()
+    units([(me + far) % n])
+    for l in range(2):
+        back[l, 1, l] = chain_start(held, flight, two, l, l)
+    for k in range(2, far + 1):
+        for short in (True, False):
+            for l in range(2):
+                side = 1 - l if short else l
+                if k <= hops_of(side, l):
+                    chain_step(held, flight, two, back, k, l, side)
+    total = chain_end(held, flight, back)
+    for c in list(chained.values()) + list(back.values()):
         c.wait_send()
-    total = own[...].astype(F32)
-    for k, c in flying:
-        c.wait()
-        total = total + r2[k].astype(F32)
     stream = gated(stream_ref[...], 5, total + downb_ref[...])
-    value = jnp.dot(modulated(stream, 6), fw_ref[...], preferred_element_type=F32) + fb_ref[...]
+    value = lax.dot_general(
+        modulated(stream, 6), fw_ref[...], (((1,), (1,)), ((), ())), preferred_element_type=F32
+    ) + fb_ref[...]
     noise[...] = value
     c = remote(noise, other, s3, q3, {"cfg": 1 - half})
     c.start()
@@ -364,14 +384,13 @@
         out_specs=vmem,
         scratch_shapes=[
             pltpu.VMEM((2, 32, GRID, D), BF16),
-            pltpu.VMEM((n, rows, D), BF16),
-            pltpu.VMEM((n, rows, D), BF16),
-            pltpu.VMEM((n, rows, D), BF16),
+            pltpu.VMEM((2, 32, GRID, D), BF16),
+            pltpu.VMEM((n, 2, GRID, D), BF16),
+            pltpu.VMEM((n, 2, GRID, D), BF16),
             pltpu.VMEM((rows, D), F32),
-            pltpu.VMEM((rows, D), BF16),
             pltpu.VMEM((rows, 16), F32),
             pltpu.VMEM((rows, 16), F32),
-        ] + [dma((32,))] * 2 + [dma((n,))] * 6 + [dma(()), dma(())],
+        ] + [dma((32,))] * 6 + [dma(()), dma(())],
         compiler_params=pltpu.CompilerParams(
             collective_id=1, has_side_effects=True, vmem_limit_bytes=60000000
         ),
@@ -397,21 +416,16 @@
     cond = jnp.dot(step_onehot, time_table, preferred_element_type=F32) + jnp.dot(
         class_onehot, label_table, preferred_element_type=F32
     )
-    mine = D // tp_n
-    cond = jnp.pad(cond, ((0, 0), (0, 2 * LANES - mine)))
-    mrows = modulation_weight.shape[0]
-    mw = jnp.transpose(modulation_weight.reshape(mrows, tp_n, mine), (1, 0, 2))
-    mw = jnp.pad(mw, ((0, 0), (0, LANES - mrows), (0, 2 * LANES - mine)))
-    mb = jnp.pad(modulation_bias, (0, LANES - mrows)).reshape(1, LANES)
     lat_t = jnp.transpose(latents.astype(BF16), (1, 2, 0))
-    mod, lat_all = conditioning(cond, mw, mb, lat_t, tp_n, rs_n)
+    mod, lat_all = conditioning(
+        cond, modulation_weight, modulation_bias.reshape(1, -1), lat_t, tp_n, rs_n
+    )
 
     row_np, col_np = position_tables()
     row, col = jnp.asarray(row_np), jnp.asarray(col_np)
     patch_bias = patch_bias.reshape(1, D)
-    fill = 2 * LANES - mine
-    w = jnp.pad(heads_weight[0], ((0, 0), (0, 0), (0, fill))).reshape(D, 6 * LANES)
-    b = jnp.pad(heads_bias[0], ((0, 0), (0, fill))).reshape(1, 6 * LANES)
+    w = jnp.transpose(heads_weight[0], (1, 2, 0))
+    b = heads_bias[0]
     partial = attention(lat_all, patch_weight, patch_bias, col, row, mod, w, b, output_weight[0])
 
     own = lax.dynamic_slice_in_dim(latents, tp * share, share, 0)
@@ -421,8 +435,9 @@
     coef = jnp.dot(hot, solver_table, precision=lax.Precision.HIGHEST)
     coef = jnp.repeat(coef, share, axis=0)
     out = feed(
-        tp_n, partial, own, patch_weight, patch_bias, col, row, mod, output_bias, up_weight[0],
-        up_bias, down_weight[0], down_bias, final_weight, final_bias.reshape(1, patch),
+        tp_n, partial, own, patch_weight, patch_bias, col, row, mod, output_bias,
+        jnp.transpose(up_weight[0]), up_bias, down_weight[0], down_bias,
+        jnp.transpose(final_weight), final_bias.reshape(1, patch),
         coef[:, 0:1], coef[:, 1:2],
     )
     kept = lax.dynamic_slice_in_dim(out, half * (patch // 2), patch // 2, 1)

time: 139 us -> 131 us (0.942)
  the two profiles are of different devices: /device:TPU:4 before, /device:TPU:2 now
where the time goes in v3:
time: 131 us; the launch traced here: 130 us
  Pallas kernels  119 us (91%)
  local copies, waits for them, and re-layouts  6.81 us (5%)
  matrix products  2.06 us (2%)
  other arithmetic  2.06 us (2%)
    pallas_call x1, Pallas kernels, feed(): pl.pallas_call(functools.partial(feed_kernel, n), out_shape=jax.ShapeDtyp...  67.7 us
    pallas_call x1, Pallas kernels, conditioning(): pl.pallas_call(functools.partial(conditioning_kernel, tp_n, rs_n), out_sh...  36.3 us
    pallas_call x1, Pallas kernels, attention(): pl.pallas_call(attention_kernel, out_shape=jax.ShapeDtypeStruct((8, 2, GR...  15.4 us

profile of v3, /device:TPU:2, one launch (start us, length us, event | category | flops | bytes accessed | tf_op | source)
XLA Modules:
  0.0 130.3 jit_solution(4434786649537286284)
XLA Ops:
  0.0 0.0 copy-start
  0.0 0.8 copy.29
  0.8 0.1 eq.67
  0.9 1.0 fusion.1
  1.9 0.7 broadcast_select_fusion
  2.6 0.1 copy.30
  2.7 0.1 select_n.32
  2.8 0.8 convolution_add_fusion.cond_ref
  3.6 1.4 %convert_bitcast_fusion.lat_ref = bf16[2,16,256]{2,1,0:T(8,128)(2,1)} fusion(f32[256,2,16]{0,2,1:T(8,128)} %param.22), kind=kLoop, calls=%fused_computation.4 | loop fusion | flops 8192 | bytes 49152 | tf_op jit(solution)/shard_map/transpose | solution.py:419
  5.0 36.3 %conditioning.1 = (f32[2,8,1152]{2,1,0:T(8,128)}, bf16[4,2,16,256]{3,2,1,0:T(8,128)(2,1)}) custom-call(f32[16,144]{1,0:T(8,128)} %convolution_add_fusion.cond_ref, bf16[36,1152]{1,0:T(8,128)(2,1)} %w_ref.1, f32[1,36]{1,0:T(1,128)} %bitcast.35, bf16[2,16,256]{2,1,0:T(8,128)(2,1)} %convert_bitcast_fusion.lat_ref), custom_call_target="tpu_custom_call" | custom-call | tf_op jit(solution)/shard_map/conditioning/pallas_call | solution.py:129
  41.3 1.3 reshape.33.pb_ref
  42.6 1.3 copy.43
  43.8 15.4 %attention.1.part_ref = bf16[8,2,32,1152]{3,2,1,0:T(8,128)(2,1)} custom-call(bf16[4,2,16,256]{3,2,1,0:T(8,128)(2,1)} %get-tuple-element.7.lat_ref, bf16[16,1152]{1,0:T(8,128)(2,1)} %pw_ref.3, f32[1,1152]{1,0:T(1,128)} %reshape.33.pb_ref, f32[32,1152]{1,0:T(8,128)} %constant.51.clone.col_ref, f32[32,1152]{1,0:T(8,128)} %constant.50.clone.row_ref, ...), custom_call_target="tpu_custom_call" | custom-call | tf_op jit(solution)/shard_map/attention/pallas_call | solution.py:207
  59.3 0.0 copy-done.1
  59.3 0.1 dynamic-slice_bitcast_fusion
  59.3 0.7 copy.31
  60.0 0.2 dynamic-slice_reduce_fusion
  60.2 0.0 copy-done.3
  60.2 0.2 fusion.3
  60.4 0.7 fusion.7
  61.1 67.7 %feed.1 = f32[64,16]{1,0:T(8,128)} custom-call(bf16[8,2,32,1152]{3,2,1,0:T(8,128)(2,1)} %attention.1.part_ref, f32[64,16]{1,0:T(8,128)} %bitcast.30, bf16[16,1152]{1,0:T(8,128)(2,1)} %pw_ref.3, f32[1,1152]{1,0:T(1,128)} %reshape.33.pb_ref, f32[32,1152]{1,0:T(8,128)} %constant.51.clone.col_ref, f32[32,1152]{1,0:T(8,128)} %constant.50.clone.row_ref, ...), custom_call_target="tpu_custom_call" | custom-call | tf_op jit(solution)/shard_map/feed/pallas_call | solution.py:380
  128.8 0.8 constant_dynamic-slice_fusion
  129.6 0.1 copy.38
  129.7 0.6 copy.36
  (6 shorter events, 0.0 us)
Async XLA Ops:
  0.0 2.8 %copy-start = (bf16[1001,144]{0,1:T(8,128)(2,1)S(1)}, bf16[1001,144]{0,1:T(8,128)(2,1)}, u32[]{:S(2)}) copy-start(bf16[1001,144]{0,1:T(8,128)(2,1)} %param.27) | copy-start | bytes 864868
  43.8 15.4 %copy-start.1 = (f32[256,2,16]{0,2,1:T(8,128)S(1)}, f32[256,2,16]{0,2,1:T(8,128)}, u32[]{:S(2)}) copy-start(f32[256,2,16]{0,2,1:T(8,128)} %param.22) | copy-start | bytes 98308
  43.8 16.2 %copy-start.2 = (s32[8,2]{0,1:T(2,128)S(1)}, s32[8,2]{0,1:T(2,128)}, u32[]{:S(2)}) copy-start(s32[8,2]{0,1:T(2,128)} %param.23) | copy-start | bytes 196
  43.8 16.4 %copy-start.3 = (f32[250,2]{0,1:T(2,128)S(1)}, f32[250,2]{0,1:T(2,128)}, u32[]{:S(2)}) copy-start(f32[250,2]{0,1:T(2,128)} %param.25) | copy-start | bytes 6004

commit v4 on v3

--- a/solution.py
+++ b/solution.py
@@ -238,40 +238,47 @@
         away = hops_of(side, l) - (k - 1)
         return (me + away) % n if side == 0 else (me - away + n) % n
 
-    def chain_start(source, flight, sems, l, side):
-        i = (side * 2 + l) * 8 + 1
-        c = remote(source.at[owner(side, l, 1), l], flight.at[1, i], sems[0].at[i], sems[1].at[i],
-                   left if side else right)
+    size = GRID // 2
+    pieces = [(l, side, p) for p in range(2) for l in range(2) for side in range(2)]
+
+    def slot(l, side, p, k):
+        return ((side * 2 + l) * 2 + p) * 4 + (k - 1)
+
+    def piece(ref, block, l, p):
+        return ref.at[block, l, pl.ds(p * size, size)]
+
+    def send(src, dst, sems, i, side):
+        c = remote(src, dst, sems[0].at[i], sems[1].at[i], left if side else right)
         c.start()
         return c
 
-    def chain_step(source, flight, sems, chained, k, l, side):
-        i = (side * 2 + l) * 8 + k
-        chained[side, k - 1, l].wait_recv()
-        flight[0, i] = (
-            flight[1, i - 1].astype(F32) + source[owner(side, l, k), l].astype(F32)
-        ).astype(BF16)
-        c = remote(flight.at[0, i], flight.at[1, i], sems[0].at[i], sems[1].at[i],
-                   left if side else right)
-        c.start()
-        chained[side, k, l] = c
-
-    def chain_end(source, flight, chained):
+    def chain_start(source, moving, sems, l, side, p):
+        i = slot(l, side, p, 1)
+        return send(piece(source, owner(side, l, 1), l, p), moving.at[1, i], sems, i, side)
+
+    def chain_step(source, moving, sems, chained, k, l, side, p):
+        i = slot(l, side, p, k)
+        chained[side, k - 1, l, p].wait_recv()
+        mine = source[owner(side, l, k), l, p * size : (p + 1) * size, :]
+        moving[0, i] = (moving[1, i - 1].astype(F32) + mine.astype(F32)).astype(BF16)
+        chained[side, k, l, p] = send(moving.at[0, i], moving.at[1, i], sems, i, side)
+
+    def chain_end(source, moving, chained):
         sums = []
         for l in range(2):
-            total = source[me, l].astype(F32)
-            for side in range(2):
-                k = hops_of(side, l)
-                chained[side, k, l].wait_recv()
-                total = total + flight[1, (side * 2 + l) * 8 + k].astype(F32)
-            sums.append(total)
+            for p in range(2):
+                total = source[me, l, p * size : (p + 1) * size, :].astype(F32)
+                for side in range(2):
+                    k = hops_of(side, l)
+                    chained[side, k, l, p].wait_recv()
+                    total = total + moving[1, slot(l, side, p, k)].astype(F32)
+                sums.append(total)
         return jnp.concatenate(sums, axis=0)
 
     one, two = (s1, q1), (s2, q2)
     chained = {}
-    for l in range(2):
-        for side in range(2):
-            chained[side, 1, l] = chain_start(part_ref, chain, one, l, side)
+    for l, side, p in pieces:
+        chained[side, 1, l, p] = chain_start(part_ref, chain, one, l, side, p)
     rows = GRID
 
     def mods(m):
@@ -299,28 +306,25 @@
         lat_ref[...].astype(BF16), pw_ref[...], preferred_element_type=F32
     ) + jnp.concatenate([place, place], axis=0)
     for k in range(2, far + 1):
-        for l in range(2):
-            for side in range(2):
-                if k <= hops_of(side, l):
-                    chain_step(part_ref, chain, one, chained, k, l, side)
+        for l, side, p in pieces:
+            if k <= hops_of(side, l):
+                chain_step(part_ref, chain, one, chained, k, l, side, p)
     total = chain_end(part_ref, chain, chained)
     stream = gated(stream_ref[...], 2, total + ob_ref[...])
     stream_ref[...] = stream
     second = modulated(stream, 3)
     gathered[me, 0], gathered[me, 1] = second[:rows], second[rows:]
 
+    hops = {}
+
     def hop(k):
-        out = []
-        for l in range(2):
-            for side in range(2):
-                if k <= hops_of(side, l):
-                    b = (me - (k - 1) + n) % n if side == 0 else (me + (k - 1)) % n
-                    i = (side * 2 + l) * 8 + k
-                    c = remote(gathered.at[b, l], gathered.at[b, l], sg.at[i], qg.at[i],
-                               left if side else right)
-                    c.start()
-                    out.append(c)
-        return out
+        for l, side, p in pieces:
+            if k > 1 and k - 1 <= hops_of(side, l):
+                hops[side, k - 1, l, p].wait_recv()
+            if k <= hops_of(side, l):
+                b = (me - (k - 1) + n) % n if side == 0 else (me + (k - 1)) % n
+                part = piece(gathered, b, l, p)
+                hops[side, k, l, p] = send(part, part, (sg, qg), slot(l, side, p, k), side)
 
     def units(blocks):
         x = jnp.concatenate([gathered[b, l] for b in blocks for l in range(2)], axis=0)
@@ -333,29 +337,27 @@
             for l in range(2):
                 held[b, l] = y[(2 * j + l) * rows : (2 * j + l + 1) * rows]
 
-    hops = hop(1)
+    hop(1)
     units([me])
     back = {}
     for k in range(1, far):
-        for c in hops:
-            c.wait()
-        hops = hop(k + 1)
+        hop(k + 1)
         units([(me - k + n) % n, (me + k) % n])
-    for l in range(2):
-        back[1 - l, 1, l] = chain_start(held, flight, two, l, 1 - l)
-    for c in hops:
-        c.wait()
+    for l, side, p in pieces:
+        if side != l:
+            back[side, 1, l, p] = chain_start(held, flight, two, l, side, p)
+    hop(far + 1)
     units([(me + far) % n])
-    for l in range(2):
-        back[l, 1, l] = chain_start(held, flight, two, l, l)
+    for l, side, p in pieces:
+        if side == l:
+            back[side, 1, l, p] = chain_start(held, flight, two, l, side, p)
     for k in range(2, far + 1):
         for short in (True, False):
-            for l in range(2):
-                side = 1 - l if short else l
-                if k <= hops_of(side, l):
-                    chain_step(held, flight, two, back, k, l, side)
+            for l, side, p in pieces:
+                if (side != l) == short and k <= hops_of(side, l):
+                    chain_step(held, flight, two, back, k, l, side, p)
     total = chain_end(held, flight, back)
-    for c in list(chained.values()) + list(back.values()):
+    for c in list(chained.values()) + list(hops.values()) + list(back.values()):
         c.wait_send()
     stream = gated(stream_ref[...], 5, total + downb_ref[...])
     value = lax.dot_general(
@@ -383,8 +385,8 @@
         in_specs=[vmem] * len(operands),
         out_specs=vmem,
         scratch_shapes=[
-            pltpu.VMEM((2, 32, GRID, D), BF16),
-            pltpu.VMEM((2, 32, GRID, D), BF16),
+            pltpu.VMEM((2, 32, GRID // 2, D), BF16),
+            pltpu.VMEM((2, 32, GRID // 2, D), BF16),
             pltpu.VMEM((n, 2, GRID, D), BF16),
             pltpu.VMEM((n, 2, GRID, D), BF16),
             pltpu.VMEM((rows, D), F32),

time: 131 us -> 123 us (0.939)
  the two profiles are of different devices: /device:TPU:2 before, /device:TPU:8 now
where the time goes in v4:
time: 123 us
  Pallas kernels  112 us (91%)
  local copies, waits for them, and re-layouts  6.81 us (6%)
  matrix products  2.06 us (2%)
  other arithmetic  2.06 us (2%)
    pallas_call x1, Pallas kernels, feed(): pl.pallas_call(functools.partial(feed_kernel, n), out_shape=jax.ShapeDtyp...  60.5 us
    pallas_call x1, Pallas kernels, conditioning(): pl.pallas_call(functools.partial(conditioning_kernel, tp_n, rs_n), out_sh...  35.8 us
    pallas_call x1, Pallas kernels, attention(): pl.pallas_call(attention_kernel, out_shape=jax.ShapeDtypeStruct((8, 2, GR...  15.4 us

profile of v4, /device:TPU:8, one launch (start us, length us, event | category | flops | bytes accessed | tf_op | source)
XLA Modules:
  0.0 122.6 jit_solution(1984908805726622173)
XLA Ops:
  0.0 0.0 copy-start
  0.0 0.8 copy.29
  0.8 0.1 eq.67
  0.9 1.0 fusion.1
  1.9 0.7 broadcast_select_fusion
  2.6 0.1 copy.30
  2.7 0.1 select_n.32
  2.8 0.0 copy-done
  2.8 0.8 convolution_add_fusion.cond_ref
  3.6 1.4 %convert_bitcast_fusion.lat_ref = bf16[2,16,256]{2,1,0:T(8,128)(2,1)} fusion(f32[256,2,16]{0,2,1:T(8,128)} %param.22), kind=kLoop, calls=%fused_computation.4 | loop fusion | flops 8192 | bytes 49152 | tf_op jit(solution)/shard_map/transpose | solution.py:421
  5.0 35.8 %conditioning.1 = (f32[2,8,1152]{2,1,0:T(8,128)}, bf16[4,2,16,256]{3,2,1,0:T(8,128)(2,1)}) custom-call(f32[16,144]{1,0:T(8,128)} %convolution_add_fusion.cond_ref, bf16[36,1152]{1,0:T(8,128)(2,1)} %w_ref.1, f32[1,36]{1,0:T(1,128)} %bitcast.35, bf16[2,16,256]{2,1,0:T(8,128)(2,1)} %convert_bitcast_fusion.lat_ref), custom_call_target="tpu_custom_call" | custom-call | tf_op jit(solution)/shard_map/conditioning/pallas_call | solution.py:129
  40.8 1.3 %reshape.33.pb_ref = f32[1,1152]{1,0:T(1,128)} reshape(f32[1152]{0:T(1024)} %param.29) | data formatting | bytes 9216 | tf_op jit(solution)/shard_map/reshape | solution.py:428
  42.1 1.3 %copy.43 = f32[1,3,144]{2,1,0:T(4,128)} copy(f32[1,3,144]{2,0,1:T(1,128)} %param.33) | data formatting | bytes 3456
  43.3 15.4 %attention.1.part_ref = bf16[8,2,32,1152]{3,2,1,0:T(8,128)(2,1)} custom-call(bf16[4,2,16,256]{3,2,1,0:T(8,128)(2,1)} %get-tuple-element.7.lat_ref, bf16[16,1152]{1,0:T(8,128)(2,1)} %pw_ref.3, f32[1,1152]{1,0:T(1,128)} %reshape.33.pb_ref, f32[32,1152]{1,0:T(8,128)} %constant.51.clone.col_ref, f32[32,1152]{1,0:T(8,128)} %constant.50.clone.row_ref, ...), custom_call_target="tpu_custom_call" | custom-call | tf_op jit(solution)/shard_map/attention/pallas_call | solution.py:207
  58.8 0.0 copy-done.1
  58.8 0.1 dynamic-slice_bitcast_fusion
  58.8 0.7 copy.31
  59.5 0.2 dynamic-slice_reduce_fusion
  59.7 0.2 fusion.3
  59.9 0.7 fusion.7
  60.6 60.5 %feed.1 = f32[64,16]{1,0:T(8,128)} custom-call(bf16[8,2,32,1152]{3,2,1,0:T(8,128)(2,1)} %attention.1.part_ref, f32[64,16]{1,0:T(8,128)} %bitcast.30, bf16[16,1152]{1,0:T(8,128)(2,1)} %pw_ref.3, f32[1,1152]{1,0:T(1,128)} %reshape.33.pb_ref, f32[32,1152]{1,0:T(8,128)} %constant.51.clone.col_ref, f32[32,1152]{1,0:T(8,128)} %constant.50.clone.row_ref, ...), custom_call_target="tpu_custom_call" | custom-call | tf_op jit(solution)/shard_map/feed/pallas_call | solution.py:382
  121.1 0.8 constant_dynamic-slice_fusion
  121.9 0.1 copy.38
  122.0 0.6 copy.36
  (6 shorter events, 0.0 us)
Async XLA Ops:
  0.0 2.8 %copy-start = (bf16[1001,144]{0,1:T(8,128)(2,1)S(1)}, bf16[1001,144]{0,1:T(8,128)(2,1)}, u32[]{:S(2)}) copy-start(bf16[1001,144]{0,1:T(8,128)(2,1)} %param.27) | copy-start | bytes 864868
  43.3 15.4 %copy-start.1 = (f32[256,2,16]{0,2,1:T(8,128)S(1)}, f32[256,2,16]{0,2,1:T(8,128)}, u32[]{:S(2)}) copy-start(f32[256,2,16]{0,2,1:T(8,128)} %param.22) | copy-start | bytes 98308
  43.3 16.2 %copy-start.2 = (s32[8,2]{0,1:T(2,128)S(1)}, s32[8,2]{0,1:T(2,128)}, u32[]{:S(2)}) copy-start(s32[8,2]{0,1:T(2,128)} %param.23) | copy-start | bytes 196
  43.3 16.4 %copy-start.3 = (f32[250,2]{0,1:T(2,128)S(1)}, f32[250,2]{0,1:T(2,128)}, u32[]{:S(2)}) copy-start(f32[250,2]{0,1:T(2,128)} %param.25) | copy-start | bytes 6004

commit v5 on v4

--- a/solution.py
+++ b/solution.py
@@ -158,7 +158,7 @@
     def project(i):
         return lax.dot_general(
             normed[...], w_ref[i], (((1,), (1,)), ((), ())), preferred_element_type=F32
-        ) + b_ref[i : i + 1, :]
+        ) + b_ref[i]
 
     def fill(latent, slot):
         emb = lax.dot_general(
@@ -372,7 +372,9 @@
     conditional = jnp.where(first, value, theirs)
     unconditional = jnp.where(first, theirs, value)
     guided = unconditional + GUIDANCE * (conditional - unconditional)
-    out_ref[...] = c0_ref[...] * lat_ref[...] + c1_ref[...] * guided
+    result = c0_ref[...] * lat_ref[...] + c1_ref[...] * guided
+    width = result.shape[1] // 2
+    out_ref[...] = jnp.where(first, result[:, :width], result[:, width:])
 
 
 def feed(n, *operands):
@@ -381,7 +383,7 @@
     rows = 2 * GRID
     return pl.pallas_call(
         functools.partial(feed_kernel, n),
-        out_shape=jax.ShapeDtypeStruct((rows, 16), F32),
+        out_shape=jax.ShapeDtypeStruct((rows, 8), F32),
         in_specs=[vmem] * len(operands),
         out_specs=vmem,
         scratch_shapes=[
@@ -427,7 +429,7 @@
     row, col = jnp.asarray(row_np), jnp.asarray(col_np)
     patch_bias = patch_bias.reshape(1, D)
     w = jnp.transpose(heads_weight[0], (1, 2, 0))
-    b = heads_bias[0]
+    b = jnp.transpose(heads_bias, (1, 0, 2))
     partial = attention(lat_all, patch_weight, patch_bias, col, row, mod, w, b, output_weight[0])
 
     own = lax.dynamic_slice_in_dim(latents, tp * share, share, 0)
@@ -442,8 +444,7 @@
         jnp.transpose(final_weight), final_bias.reshape(1, patch),
         coef[:, 0:1], coef[:, 1:2],
     )
-    kept = lax.dynamic_slice_in_dim(out, half * (patch // 2), patch // 2, 1)
-    return jnp.transpose(kept.reshape(latents_dev, share, patch // 2), (1, 0, 2))
+    return jnp.transpose(out.reshape(latents_dev, share, patch // 2), (1, 0, 2))
 
 
 def solution(mesh):

time: 123 us -> 122 us (level)
  local copies, waits for them, and re-layouts: 6.81 us -> 5.43 us
    reshape x1, local copies, waits for them, and re-layouts: 0.08 us -> 1.43 us  [per_device(): return jnp.transpose(out.reshape(latents_dev, share, patch // 2), (1, 0, 2))]
    unnamed x10 -> x9, local copies, waits for them, and re-layouts: 2.09 us -> 0.81 us
where the time goes in v5:
time: 122 us; the launch traced here: 121 us
  Pallas kernels  112 us (92%)
  local copies, waits for them, and re-layouts  5.43 us (4%)
  matrix products  2.06 us (2%)
  other arithmetic  2.06 us (2%)
    pallas_call x1, Pallas kernels, feed(): pl.pallas_call(functools.partial(feed_kernel, n), out_shape=jax.ShapeDtyp...  60.5 us
    pallas_call x1, Pallas kernels, conditioning(): pl.pallas_call(functools.partial(conditioning_kernel, tp_n, rs_n), out_sh...  35.8 us
    pallas_call x1, Pallas kernels, attention(): pl.pallas_call(attention_kernel, out_shape=jax.ShapeDtypeStruct((8, 2, GR...  15.5 us

profile of v5, /device:TPU:8, one launch (start us, length us, event | category | flops | bytes accessed | tf_op | source)
XLA Modules:
  0.0 121.4 jit_solution(8906091551631189531)
XLA Ops:
  0.0 0.0 copy-start
  0.0 0.8 copy.30
  0.8 0.1 eq.67
  0.9 1.0 fusion.1
  1.9 0.7 broadcast_select_fusion
  2.6 0.1 copy.31
  2.7 0.1 select_n.29
  2.8 0.0 copy-done
  2.8 0.8 convolution_add_fusion.cond_ref
  3.6 1.4 %convert_bitcast_fusion.lat_ref = bf16[2,16,256]{2,1,0:T(8,128)(2,1)} fusion(f32[256,2,16]{0,2,1:T(8,128)} %param.22), kind=kLoop, calls=%fused_computation.4 | loop fusion | flops 8192 | bytes 49152 | tf_op jit(solution)/shard_map/transpose | solution.py:423
  5.0 35.8 %conditioning.1 = (f32[2,8,1152]{2,1,0:T(8,128)}, bf16[4,2,16,256]{3,2,1,0:T(8,128)(2,1)}) custom-call(f32[16,144]{1,0:T(8,128)} %convolution_add_fusion.cond_ref, bf16[36,1152]{1,0:T(8,128)(2,1)} %w_ref.1, f32[1,36]{1,0:T(1,128)} %bitcast.32, bf16[2,16,256]{2,1,0:T(8,128)(2,1)} %convert_bitcast_fusion.lat_ref), custom_call_target="tpu_custom_call" | custom-call | tf_op jit(solution)/shard_map/conditioning/pallas_call | solution.py:129
  40.8 1.3 %reshape.33.pb_ref = f32[1,1152]{1,0:T(1,128)} reshape(f32[1152]{0:T(1024)} %param.29) | data formatting | bytes 9216 | tf_op jit(solution)/shard_map/reshape | solution.py:430
  42.1 0.0 copy-start.1
  42.1 15.5 %attention.1.part_ref = bf16[8,2,32,1152]{3,2,1,0:T(8,128)(2,1)} custom-call(bf16[4,2,16,256]{3,2,1,0:T(8,128)(2,1)} %get-tuple-element.7.lat_ref, bf16[16,1152]{1,0:T(8,128)(2,1)} %pw_ref.3, f32[1,1152]{1,0:T(1,128)} %reshape.33.pb_ref, f32[32,1152]{1,0:T(8,128)} %constant.48.clone.col_ref, f32[32,1152]{1,0:T(8,128)} %constant.47.clone.row_ref, ...), custom_call_target="tpu_custom_call" | custom-call | tf_op jit(solution)/shard_map/attention/pallas_call | solution.py:207
  57.6 0.0 copy-done.1
  57.6 0.1 dynamic-slice_bitcast_fusion
  57.6 0.7 copy.32
  58.3 0.0 copy-done.2
  58.3 0.2 dynamic-slice_reduce_fusion
  58.5 0.0 copy-done.3
  58.5 0.2 fusion.3
  58.7 0.7 fusion.7
  59.4 60.5 %feed.1 = f32[64,8]{1,0:T(8,128)} custom-call(bf16[8,2,32,1152]{3,2,1,0:T(8,128)(2,1)} %attention.1.part_ref, f32[64,16]{1,0:T(8,128)} %bitcast.29, bf16[16,1152]{1,0:T(8,128)(2,1)} %pw_ref.3, f32[1,1152]{1,0:T(1,128)} %reshape.33.pb_ref, f32[32,1152]{1,0:T(8,128)} %constant.48.clone.col_ref, f32[32,1152]{1,0:T(8,128)} %constant.47.clone.row_ref, ...), custom_call_target="tpu_custom_call" | custom-call | tf_op jit(solution)/shard_map/feed/pallas_call | solution.py:384
  119.9 1.4 %copy.36 = f32[2,32,8]{1,2,0:T(8,128)} copy(f32[2,32,8]{2,1,0:T(8,128)} %bitcast.28) | data formatting | bytes 4096 | tf_op jit(solution)/shard_map/reshape | solution.py:447
  (3 shorter events, 0.0 us)
Async XLA Ops:
  0.0 2.8 %copy-start = (bf16[1001,144]{0,1:T(8,128)(2,1)S(1)}, bf16[1001,144]{0,1:T(8,128)(2,1)}, u32[]{:S(2)}) copy-start(bf16[1001,144]{0,1:T(8,128)(2,1)} %param.27) | copy-start | bytes 864868
  42.1 15.5 %copy-start.1 = (f32[256,2,16]{0,2,1:T(8,128)S(1)}, f32[256,2,16]{0,2,1:T(8,128)}, u32[]{:S(2)}) copy-start(f32[256,2,16]{0,2,1:T(8,128)} %param.22) | copy-start | bytes 98308
  42.1 16.3 %copy-start.2 = (s32[8,2]{0,1:T(2,128)S(1)}, s32[8,2]{0,1:T(2,128)}, u32[]{:S(2)}) copy-start(s32[8,2]{0,1:T(2,128)} %param.23) | copy-start | bytes 196
  42.1 16.5 %copy-start.3 = (f32[250,2]{0,1:T(2,128)S(1)}, f32[250,2]{0,1:T(2,128)}, u32[]{:S(2)}) copy-start(f32[250,2]{0,1:T(2,128)} %param.25) | copy-start | bytes 6004
